TPU v7x, 128 devices: a whole 4x4x4 slice. The times are simulated.
128 devices in a mesh: row: 8 (over x_lo, z), col: 16 (over x_hi, y, core).
Axes of the slice: x: 4 (x_hi: 2, x_lo: 2; x = x_hi * 2 + x_lo), y: 4, z: 4, core: 2. Of those that a mesh axis runs over, the one named last changes fastest.
Arguments:
- child_rhs: bfloat16 [2, 16384, 256], P(None, 'row', 'col'), may hold values from -6 to 6
- child_inverse_t: bfloat16 [2, 16384, 8192], P(None, 'row', 'col'), may hold values from -0.046875 to 0.046875
- boundary_tiles: bfloat16 [2, 16384, 8192], P(None, 'row', 'col'), may hold values from -0.046875 to 0.046875
- boundary_lists: int32 [2, 64], replicated, may hold values from 0 to 95, as said below
- root_rhs: bfloat16 [2, 12288, 256], P(None, 'col'), may hold values from -6 to 6
- root_inverse: bfloat16 [2, 12288, 12288], P(None, 'row', 'col'), may hold values from -0.0390625 to 0.0390625
Outputs:
- child_solution: bfloat16 [2, 8192, 512], P(None, 'col', 'row')
- root_solution: float32 [2, 12288, 256], P(None, 'row', 'col')
Inputs may be any that keep to these rules, and one draw needn't show every extreme that they name: `boundary_lists`: within one child the 64 entries name distinct root blocks; the two children together name every one of the 96 root blocks.
All inputs are finite; a program needn't handle non-finite values.
Results may differ from a plain program's by a relative error of at most 0.0055.
Values may be sent and summed in bfloat16 or wider, within the bound.
A program may use at most 128 MiB of HBM per device.

v0:
```python
import jax
import jax.numpy as jnp
from jax import lax
from jax.sharding import PartitionSpec as P

BLK = 128


def swapped(x, axis, distance):
    return lax.ppermute(x, axis, [(i, i ^ 1 << distance) for i in range(lax.axis_size(axis))])


def turned_dot(left, right):
    return lax.dot_general(
        left, right, (((0,), (0,)), ((), ())), preferred_element_type=jnp.float32
    )


def plain_dot(left, right):
    return jnp.dot(left, right, preferred_element_type=jnp.float32)


def complex_turned(left, right):
    real_part = turned_dot(left[0], right[0]) - turned_dot(left[1], right[1])
    imag_part = turned_dot(left[0], right[1]) + turned_dot(left[1], right[0])
    return (real_part, imag_part)


def complex_plain(left, right):
    real_part = plain_dot(left[0], right[0]) - plain_dot(left[1], right[1])
    imag_part = plain_dot(left[0], right[1]) + plain_dot(left[1], right[0])
    return (real_part, imag_part)


def local(child_rhs, child_inverse_t, boundary_tiles, boundary_lists, root_rhs, root_inverse):
    real_part, imag_part = complex_turned(
        child_inverse_t, lax.all_gather(child_rhs, "col", axis=2, tiled=True)
    )
    partial_child = jnp.stack((real_part, imag_part))
    half_size = lax.axis_size("row") // 2
    levels = half_size.bit_length() - 1
    quarter_index = lax.axis_index("row") % half_size
    col_share = partial_child.shape[2] // half_size
    current = partial_child
    for bit_level in range(levels):
        current = current + swapped(current, "row", bit_level)
    full_solution = current.astype(jnp.bfloat16)
    own_solution = lax.dynamic_slice_in_dim(full_solution, quarter_index * col_share, col_share, 2)
    tile_real = boundary_tiles[0]
    tile_imag = boundary_tiles[1]
    real_part, imag_part = complex_plain((tile_real, tile_imag), full_solution)
    update = lax.psum_scatter(
        jnp.stack((real_part, imag_part), axis=1), "col", scatter_dimension=0, tiled=True
    ).astype(jnp.bfloat16)
    local_blocks = root_rhs.shape[1] // BLK
    col_first = lax.axis_index("col") * local_blocks
    block_table = boundary_lists.reshape(-1)
    table_ids = jnp.arange(block_table.shape[0], dtype=jnp.int32)
    block_slots = jnp.arange(local_blocks, dtype=jnp.int32)
    portion = lax.all_gather(update, ("row", "col"), axis=0, tiled=True)
    block_count = portion.shape[0] // BLK
    global_ids = jnp.arange(block_count, dtype=jnp.int32)
    matches = global_ids[:, None] == table_ids[None, :]
    targets = jnp.sum(jnp.where(matches, block_table[None, :], 0), axis=1)
    selector = (targets[None, :] - col_first == block_slots[:, None]).astype(jnp.bfloat16)
    blocks = portion.reshape(block_count, BLK, 2, portion.shape[2])
    assembled = jnp.einsum("st,tbcn->csbn", selector, blocks, preferred_element_type=jnp.float32)
    root_right = (root_rhs.astype(jnp.float32) - assembled.reshape(root_rhs.shape)).astype(
        jnp.bfloat16
    )
    root_real, root_imag = complex_plain(root_inverse, root_right)
    root_solution = lax.psum_scatter(
        jnp.stack((root_real, root_imag)), "col", scatter_dimension=2, tiled=True
    )
    return (own_solution, root_solution)


def solution(mesh):
    return jax.shard_map(
        local,
        mesh=mesh,
        in_specs=(
            P(None, "row", "col"),
            P(None, "row", "col"),
            P(None, "row", "col"),
            P(),
            P(None, "col", None),
            P(None, "row", "col"),
        ),
        out_specs=(P(None, "col", "row"), P(None, "row", "col")),
        check_vma=False,
    )
```

profile of v0, /device:TPU:0, one launch (start us, length us, event | category | flops | bytes accessed | tf_op | source)
XLA Modules:
  0.0 556.1 jit_solution(6324646950402062723)
XLA Ops:
  7.2 0.0 all-gather.3.cloned.1.call-start
  7.2 0.7 all-gather.3.cloned.1.call-update
  7.9 0.0 reduce-scatter.3.cloned.1.call-start
  7.9 52.5 %all-gather.3.cloned.1.call-done = bf16[2,2048,256]{1,2,0:T(8,128)(2,1)} async-done(((bf16[2,2048,16]{1,2,0:T(8,128)(2,1)}), bf16[2,2048,256]{1,2,0:T(8,128)(2,1)}) %all-gather.3.cloned.1.call-update) | async-done | bytes 2097168 | tf_op jit(solution)/shard_map/all_gather | solution.py:37
  60.5 0.0 copy-start.1
  60.5 2.8 fusion.16
  63.2 0.4 copy-done.1
  63.6 0.0 copy-start.2
  63.6 2.1 fusion.18
  65.7 0.0 copy-done.2
  65.7 0.7 fusion.46
  66.4 0.7 fusion.40
  67.1 0.1 pad_maximum_fusion.2
  67.2 1.6 collective-permute-start
  68.8 23.7 %collective-permute-done = f32[2,512,256]{1,2,0:T(8,128)S(1)} collective-permute-done((f32[2,512,256]{1,2,0:T(8,128)S(1)}, f32[2,512,256]{1,2,0:T(8,128)S(1)}, u32[]{:S(2)}, u32[]{:S(2)}) %collective-permute-start) | collective-permute-done | bytes 1048608 | tf_op jit(solution)/shard_map/ppermute | solution.py:10
  92.6 0.0 copy-start
  92.6 0.2 fusion.52
  92.8 3.2 collective-permute-start.1
  96.0 22.8 %collective-permute-done.1 = f32[2,512,256]{1,2,0:T(8,128)S(1)} collective-permute-done((f32[2,512,256]{1,2,0:T(8,128)S(1)}, f32[2,512,256]{1,2,0:T(8,128)S(1)}, u32[]{:S(2)}, u32[]{:S(2)}) %collective-permute-start.1) | collective-permute-done | bytes 1048608 | tf_op jit(solution)/shard_map/ppermute | solution.py:10
  118.8 0.4 add_convert_fusion
  119.2 0.0 copy-done
  119.2 0.7 fusion.10
  120.0 0.7 fusion.12
  120.7 0.7 fusion.2
  121.5 0.7 fusion.3
  122.2 2.2 pad_maximum_fusion
  124.4 0.0 copy-start.3
  124.4 0.0 reduce-scatter.3.cloned.1.call-update
  124.5 0.0 all-gather.5.cloned.1.call-start
  124.5 79.6 %reduce-scatter.3.cloned.1.call-done = f32[128,2,256]{0,2,1:T(8,128)} async-done(((f32[2048,2,256]{0,2,1:T(8,128)}), f32[128,2,256]{0,2,1:T(8,128)}) %reduce-scatter.3.cloned.1.call-update) | async-done | bytes 262160 | tf_op jit(solution)/shard_map/reduce_scatter | solution.py:52
  204.2 1.6 convert_element_type.15
  205.8 0.0 all-gather.5.cloned.1.call-update
  205.8 0.2 reduce-scatter.5.cloned.1.call-start
  206.0 0.0 copy-done.3
  206.0 0.1 broadcast_in_dim.18
  206.1 0.1 select_reduce_fusion
  206.2 246.4 %all-gather.5.cloned.1.call-done = bf16[16384,2,256]{0,2,1:T(8,128)(2,1)} async-done(((bf16[128,2,256]{0,2,1:T(8,128)(2,1)}), bf16[16384,2,256]{0,2,1:T(8,128)(2,1)}) %all-gather.5.cloned.1.call-update) | async-done | bytes 16777232 | tf_op jit(solution)/shard_map/all_gather | solution.py:60
  452.7 9.8 %copy.13 = bf16[64,8,128,128]{3,2,1,0:T(8,128)(2,1)S(1)} copy(bf16[64,8,128,128]{3,1,2,0:T(8,128)(2,1)} %bitcast.101) | data formatting | bytes 33554432
  462.5 2.3 convolution_bitcast_fusion
  464.7 0.0 slice-start
  464.7 1.6 copy.11
  466.4 0.0 slice-start.1
  466.4 1.9 fusion.36
  468.3 2.5 fusion.6
  470.8 0.0 slice-done
  470.8 0.0 slice-done.1
  470.9 0.8 fusion.8
  471.7 0.8 fusion.1
  472.5 0.8 fusion
  473.4 1.8 pad_maximum_fusion.1
  475.2 0.0 reduce-scatter.5.cloned.1.call-update
  475.3 0.7 constant_dynamic-slice_fusion
  476.0 73.7 %reduce-scatter.5.cloned.1.call-done = f32[2,1536,16]{1,2,0:T(8,128)} async-done(((f32[2,1536,256]{1,2,0:T(8,128)}), f32[2,1536,16]{1,2,0:T(8,128)}) %reduce-scatter.5.cloned.1.call-update) | async-done | bytes 196624 | tf_op jit(solution)/shard_map/reduce_scatter | solution.py:72
  (2 shorter events, 0.0 us)
Async XLA Ops:
  7.2 53.3 %all-gather.3.cloned.1.call-start = ((), (), s32[]{:S(2)}) async-start(), calls=%async_computation.2 | async-start | bytes 2228224 | tf_op jit(solution)/shard_map/all_gather | solution.py:37
  7.9 196.3 %reduce-scatter.3.cloned.1.call-start = ((), (), s32[]{:S(2)}) async-start(), calls=%async_computation.3 | async-start | bytes 4456448 | tf_op jit(solution)/shard_map/reduce_scatter | solution.py:52
  60.5 3.1 copy-start.1
  63.6 2.1 copy-start.2
  67.2 25.4 %collective-permute-start = (f32[2,512,256]{1,2,0:T(8,128)S(1)}, f32[2,512,256]{1,2,0:T(8,128)S(1)}, u32[]{:S(2)}, u32[]{:S(2)}) collective-permute-start(f32[2,512,256]{1,2,0:T(8,128)S(1)} %pad_maximum_fusion.2), channel_id=1, source_target_pairs={{0,16},{16,0},{32,48},{48,32},{64,80},{80,64},{96,112},{112,96},{1... | collective-permute-start | bytes 3145736 | tf_op jit(solution)/shard_map/ppermute | solution.py:10
  92.6 26.6 %copy-start = (bf16[2,2048,512]{2,1,0:T(8,128)(2,1)S(1)}, bf16[2,2048,512]{2,1,0:T(8,128)(2,1)}, u32[]{:S(2)}) copy-start(bf16[2,2048,512]{2,1,0:T(8,128)(2,1)} %param.8) | copy-start | bytes 12582916
  92.8 26.0 %collective-permute-start.1 = (f32[2,512,256]{1,2,0:T(8,128)S(1)}, f32[2,512,256]{1,2,0:T(8,128)S(1)}, u32[]{:S(2)}, u32[]{:S(2)}) collective-permute-start(f32[2,512,256]{1,2,0:T(8,128)S(1)} %fusion.52), channel_id=1, source_target_pairs={{0,32},{16,48},{32,0},{48,16},{64,96},{80,112},{96,64},{112,80},{1... | collective-permute-start | bytes 3145736 | tf_op jit(solution)/shard_map/ppermute | solution.py:10
  124.4 81.6 %copy-start.3 = (s32[2,64]{1,0:T(2,128)S(1)}, s32[2,64]{1,0:T(2,128)}, u32[]{:S(2)}) copy-start(s32[2,64]{1,0:T(2,128)} %param.9) | copy-start | bytes 1540
  124.5 328.2 %all-gather.5.cloned.1.call-start = ((), (), s32[]{:S(2)}) async-start(), calls=%async_computation.4 | async-start | bytes 16908288 | tf_op jit(solution)/shard_map/all_gather | solution.py:60
  205.8 343.8 %reduce-scatter.5.cloned.1.call-start = ((), (), s32[]{:S(2)}) async-start(), calls=%async_computation.5 | async-start | bytes 3342336 | tf_op jit(solution)/shard_map/reduce_scatter | solution.py:72
  464.7 6.1 %slice-start = ((s8[4718592]{0:T(1024)(128)(4,1)}), s8[524288]{0:T(1024)(128)(4,1)S(1)}, s32[]{:S(2)}) async-start(s8[4718592]{0:T(1024)(128)(4,1)} %bitcast.102), calls=%async_computation.6 | async-start | bytes 1048576
  466.4 4.5 slice-start.1
Sparse Core Ops, SparseCore 0:
  10.5 49.9 all-gather.2
  124.6 79.5 reduce-scatter.2
  206.4 246.2 all-gather.4
  475.4 74.1 reduce-scatter.4
where the time goes:
time: 556 us
  waiting for transfers between devices  499 us (90%)
  matrix products  16.5 us (3%)
  between operations  14 us (3%)
  local copies, waits for them, and re-layouts  12.6 us (2%)
  other arithmetic  8.4 us (2%)
    all_gather x1, waiting for transfers between devices, local(): portion = lax.all_gather(update, ('row', 'col'), axis=0, tiled=True)  246 us
    reduce_scatter x1, waiting for transfers between devices, local(): lax.psum_scatter(jnp.stack((real_part, imag_part), axis=1), 'col', scatte...  79.6 us
    reduce_scatter x1, waiting for transfers between devices, local(): lax.psum_scatter(jnp.stack((root_real, root_imag)), 'col', scatter_dimens...  73.7 us
    all_gather x1, waiting for transfers between devices, local(): lax.all_gather(child_rhs, 'col', axis=2, tiled=True)  52.5 us
    ppermute x2, waiting for transfers between devices, swapped(): lax.ppermute(x, axis, [(i, i ^ 1 << distance) for i in range(lax.axis_siz...  46.5 us
  transfers between devices with their start and end apart: 6, of which 6 were waited for; matrix products, arithmetic and copies ran while one was open for 0% of the time, Pallas kernels for 0%

commit v1 on v0

v1 whole, which is shorter than its diff:
```python
import functools

import jax
import jax.numpy as jnp
from jax import lax
from jax.experimental import pallas as pl
from jax.experimental.pallas import tpu as pltpu
from jax.sharding import PartitionSpec as P

MESH = pl.DeviceIdType.MESH
F32 = jnp.float32
BF16 = jnp.bfloat16
N_SEMS = 128
BLK = 128
TILE = 256


class Wire:
    def __init__(self, send_sems, recv_sems, here):
        self.send_sems, self.recv_sems, self.here = send_sems, recv_sems, here
        self.count = 0
        self.started = []

    def send(self, src, dst, device):
        at = self.count
        self.count += 1
        copy = pltpu.make_async_remote_copy(
            src_ref=src, dst_ref=dst, send_sem=self.send_sems.at[at], recv_sem=self.recv_sems.at[at],
            device_id=device, device_id_type=MESH,
        )
        copy.start()
        self.started.append(copy)
        return at

    def recv(self, at, dst):
        pltpu.make_async_remote_copy(
            src_ref=dst, dst_ref=dst, send_sem=self.send_sems.at[at], recv_sem=self.recv_sems.at[at],
            device_id=self.here, device_id_type=MESH,
        ).wait_recv()

    def drain(self):
        for copy in self.started:
            copy.wait_send()


class Ring:
    def __init__(self, me, up_device, down_device):
        self.me = me
        self.up, self.down, self.far = lax.rem(me + 1, 4), lax.rem(me + 3, 4), lax.rem(me + 2, 4)
        self.up_device, self.down_device = up_device, down_device


class Gather:
    def __init__(self, wire, ring, piece, source=None):
        self.wire, self.ring, self.piece = wire, ring, piece
        self.source = source or (lambda half: piece(half, ring.me))

    def start_half(self, half):
        w, r, piece = self.wire, self.ring, self.piece
        src = self.source(half)
        ahead, behind = (r.up_device, r.down_device) if half == 0 else (r.down_device, r.up_device)
        a = w.send(src, piece(half, r.me), ahead)
        b = w.send(src, piece(half, r.me), behind)
        if half == 0:
            self.a0, self.b0 = a, b
        else:
            self.a1, self.b1 = a, b

    def start(self):
        self.start_half(0)
        self.start_half(1)

    def forward(self):
        w, r, piece = self.wire, self.ring, self.piece
        w.recv(self.a0, piece(0, r.down))
        self.f0 = w.send(piece(0, r.down), piece(0, r.down), r.up_device)
        w.recv(self.a1, piece(1, r.up))
        self.f1 = w.send(piece(1, r.up), piece(1, r.up), r.down_device)

    def finish(self):
        w, r, piece = self.wire, self.ring, self.piece
        w.recv(self.b0, piece(0, r.up))
        w.recv(self.b1, piece(1, r.down))
        w.recv(self.f0, piece(0, r.far))
        w.recv(self.f1, piece(1, r.far))


class Reduce:
    def __init__(self, wire, ring, part, out, first, last):
        self.wire, self.ring, self.part, self.out, self.first, self.last = wire, ring, part, out, first, last

    def start(self):
        w, r, out = self.wire, self.ring, self.out
        out[0] = self.part(0, r.far).astype(BF16)
        self.i0 = w.send(out.at[0], self.first.at[0], r.up_device)
        out[1] = self.part(1, r.far).astype(BF16)
        self.i1 = w.send(out.at[1], self.first.at[1], r.down_device)
        out[2] = self.part(1, r.up).astype(BF16)
        self.i2 = w.send(out.at[2], self.last.at[0], r.up_device)
        out[3] = self.part(0, r.down).astype(BF16)
        self.i3 = w.send(out.at[3], self.last.at[1], r.down_device)

    def middle(self):
        w, r, out = self.wire, self.ring, self.out
        w.recv(self.i0, self.first.at[0])
        out[4] = (self.part(0, r.up) + self.first[0].astype(F32)).astype(BF16)
        self.i4 = w.send(out.at[4], self.last.at[2], r.up_device)
        w.recv(self.i1, self.first.at[1])
        out[5] = (self.part(1, r.down) + self.first[1].astype(F32)).astype(BF16)
        self.i5 = w.send(out.at[5], self.last.at[3], r.down_device)

    def finish(self, half):
        w, r, last = self.wire, self.ring, self.last
        if half == 0:
            w.recv(self.i3, last.at[1])
            w.recv(self.i4, last.at[2])
            return self.part(0, r.me) + last[1].astype(F32) + last[2].astype(F32)
        w.recv(self.i2, last.at[0])
        w.recv(self.i5, last.at[3])
        return self.part(1, r.me) + last[0].astype(F32) + last[3].astype(F32)


def nt_dot(left, right):
    return lax.dot_general(left, right, (((1,), (1,)), ((), ())), preferred_element_type=F32)


def nn_dot(left, right):
    return jnp.dot(left, right, preferred_element_type=F32)


def iota(shape, axis):
    return lax.broadcasted_iota(jnp.int32, shape, axis).astype(F32)


def split_by(value, size):
    quotient = jnp.floor((value + 0.5) * (1.0 / size))
    return quotient, value - quotient * size


def kernel(
    b_ref, a_hbm, f_hbm, lists_ref, rhs_ref, g_hbm, out1_ref, out2_ref,
    a_buf, f_buf, g_buf, b_all, b_neg, b_relay,
    y_part, y_out, y_first, y_last, y_all, y_lhs, y_neg, y_swap,
    u_part, u_out, u_first, u_last, u_own, u_cross, u_relay, u_got, u_flat, u_send,
    s4_in, s4_out, rr, rr_flat, onehot, rhs_t, rhs_send, r_lhs, r_neg,
    v_part, v_out, v_first, v_last, v_own, v_cross, v_relay, v_got,
    send_sems, recv_sems, local_sems,
):
    row, col = lax.axis_index("row"), lax.axis_index("col")
    x_lo, z = lax.div(row, 4), lax.rem(row, 4)
    slot, core = lax.div(col, 2), lax.rem(col, 2)
    x_hi, y = lax.div(slot, 4), lax.rem(slot, 4)
    x = x_hi * 2 + x_lo
    other = 1 - core

    def device(x, y, z, core):
        return (lax.rem(x, 2) * 4 + z, lax.div(x, 2) * 8 + y * 2 + core)

    x_up, x_down = lax.rem(x + 1, 4), lax.rem(x + 3, 4)
    up_x, down_x = device(x_up, y, z, core), device(x_down, y, z, core)
    side_x = device(x_hi * 2 + 1 - x_lo, y, z, core)
    partner = (row, slot * 2 + other)
    y_ring = Ring(y, device(x, lax.rem(y + 1, 4), z, core), device(x, lax.rem(y + 3, 4), z, core))
    z_ring = Ring(z, device(x, y, lax.rem(z + 1, 4), core), device(x, y, lax.rem(z + 3, 4), core))

    def row_peer(step):
        return lax.rem(row + step, 8)

    def slot_peer(step):
        return lax.rem(slot + step, 8)

    own_a = pltpu.make_async_copy(a_hbm, a_buf.at[core], local_sems.at[0])
    own_f = pltpu.make_async_copy(f_hbm, f_buf.at[core], local_sems.at[1])
    own_g = pltpu.make_async_copy(g_hbm, g_buf.at[core], local_sems.at[2])
    own_a.start()

    barrier = pltpu.get_barrier_semaphore()
    greet = [partner, up_x, down_x]
    greet += [(row_peer(step), col) for step in range(1, 8)]
    greet += [(row, slot_peer(step) * 2 + core) for step in range(1, 8)]
    for peer in greet:
        pl.semaphore_signal(barrier, inc=1, device_id=peer, device_id_type=MESH)
    pl.semaphore_wait(barrier, len(greet))

    wire = Wire(send_sems, recv_sems, (row, col))

    def b_piece(x_half):
        return lambda half, place: b_all.at[half, x_half * 4 + place]

    near = Gather(wire, y_ring, b_piece(x_hi), source=lambda half: b_ref.at[half])
    b_x0 = wire.send(b_ref.at[0], b_relay.at[0], up_x)
    b_x1 = wire.send(b_ref.at[1], b_relay.at[1], down_x)
    near.start()
    a_got = wire.send(a_hbm, a_buf.at[core], partner)
    b_all[:, pl.ds(slot, 1)] = b_ref[...].reshape(2, 1, 16, b_ref.shape[2])

    rows, cols = onehot.shape
    t_block, t_rest = split_by(iota((rows, cols), 0), 48)
    t_col, t_at = split_by(t_rest, 12)
    s_chip, s_rest = split_by(iota((rows, cols), 1), 64)
    s_col, _ = split_by(s_rest, 16)
    e_chip, e_rest = split_by(iota((64, cols), 1), 64)
    _, e_at = split_by(e_rest, 16)
    _, e_z = split_by(e_chip, 4)
    spread = (e_z * 16 + e_at == iota((64, cols), 0)).astype(BF16)
    spread_lists = nn_dot(lists_ref[...].astype(F32).astype(BF16), spread)
    source_list = jnp.where(iota((1, cols), 1) < cols // 2, spread_lists[0:1], spread_lists[1:2])
    onehot[...] = jnp.where(
        (t_col == s_col) & (source_list == t_block * 12 + t_at), 1.0, 0.0
    ).astype(BF16)

    pick_slot, pick_rest = split_by(iota((128, 256), 0), 16)
    for mine in (False, True):
        parity = (core if mine else other).astype(F32)
        pick = (pick_slot * 32 + parity * 16 + pick_rest == iota((128, 256), 1)).astype(BF16)
        for plane in range(2):
            turned = nt_dot(pick, rhs_ref[plane]).astype(BF16)
            if mine:
                rhs_t[pl.ds(core, 1), plane] = turned[None]
            else:
                rhs_send[plane] = turned

    own_a.wait()
    own_f.start()

    x_up_hi, x_down_hi = lax.div(x_up, 2), lax.div(x_down, 2)
    wire.recv(b_x0, b_relay.at[0])
    b_x2 = wire.send(b_relay.at[0], b_all.at[0, x_down_hi * 4 + y], up_x)
    wire.recv(b_x1, b_relay.at[1])
    b_x3 = wire.send(b_relay.at[1], b_all.at[1, x_up_hi * 4 + y], down_x)
    near.forward()
    away = Gather(wire, y_ring, b_piece(1 - x_hi))
    wire.recv(b_x2, b_all.at[0, (1 - x_hi) * 4 + y])
    away.start_half(0)
    wire.recv(b_x3, b_all.at[1, (1 - x_hi) * 4 + y])
    away.start_half(1)
    near.finish()
    away.forward()
    away.finish()
    wire.recv(a_got, a_buf.at[other])
    f_got = wire.send(f_hbm, f_buf.at[core], partner)
    rhs_got = wire.send(rhs_send, rhs_t.at[core], partner)
    own_f.wait()
    own_g.start()

    b_neg[0:128] = -b_all[1].reshape(128, b_ref.shape[2])
    b_neg[128:256] = b_all[0].reshape(128, b_ref.shape[2])

    per_q = a_buf.shape[3] // TILE

    def s1_tile(at, carry):
        q, tile = lax.div(at, per_q), lax.rem(at, per_q)
        lanes = pl.ds(pl.multiple_of(tile * TILE, TILE), TILE)
        value = nn_dot(b_all[...].reshape(256, b_ref.shape[2]), a_buf[q, 0, :, lanes])
        value += nn_dot(b_neg[...], a_buf[q, 1, :, lanes])
        where = pl.ds(pl.multiple_of(at * TILE, TILE), TILE)
        y_part[:, :, :, where] = value.reshape(2, 4, 32, TILE)
        return carry

    lax.fori_loop(0, 2 * per_q, s1_tile, 0)

    y_sum = Reduce(wire, z_ring, lambda half, place: y_part[half, place], y_out, y_first, y_last)
    y_sum.start()
    y_sum.middle()
    y_all[0, pl.ds(z, 1)] = y_sum.finish(0).astype(BF16)[None]
    y_gather = Gather(wire, z_ring, lambda half, place: y_all.at[half, place])
    y_gather.start_half(0)
    y_all[1, pl.ds(z, 1)] = y_sum.finish(1).astype(BF16)[None]
    y_gather.start_half(1)
    y_gather.forward()
    y_gather.finish()
    own_cols = pl.ds(pl.multiple_of(core * 512, 512), 512)
    other_cols = pl.ds(pl.multiple_of(other * 512, 512), 512)
    swap_got = wire.send(y_all.at[:, z, :, other_cols], y_swap, partner)
    wire.recv(f_got, f_buf.at[other])
    g_got = wire.send(g_hbm, g_buf.at[core], partner)
    own_g.wait()

    for q in range(2):
        y_re = y_all[0, :, :, q * 512:(q + 1) * 512].reshape(128, 512)
        y_im = y_all[1, :, :, q * 512:(q + 1) * 512].reshape(128, 512)
        y_lhs[q, 0:128] = y_re
        y_lhs[q, 128:256] = y_im
        y_neg[q, 0:128] = -y_im
        y_neg[q, 128:256] = y_re

    def scatter_columns(lhs, neg, weights, part, out, first, last, own, cross, relay, got):
        chunks = part.shape[0]
        tiles = part.shape[-1] // TILE
        sums = []
        for chunk in range(chunks):
            def tile_step(at, carry, chunk=chunk):
                src = pl.ds(pl.multiple_of((chunk * tiles + at) * TILE, TILE), TILE)
                value = nt_dot(lhs[0], weights[0, 0, src, :])
                value += nt_dot(neg[0], weights[0, 1, src, :])
                value += nt_dot(lhs[1], weights[1, 0, src, :])
                value += nt_dot(neg[1], weights[1, 1, src, :])
                where = pl.ds(pl.multiple_of(at * TILE, TILE), TILE)
                part[chunk, :, :, :, :, where] = value.reshape(2, 2, 4, 16, TILE)
                return carry

            lax.fori_loop(0, tiles, tile_step, 0)

            def term(half, place, chunk=chunk):
                return part[chunk, :, (x_hi if half == 1 else 1 - x_hi), place]

            total = Reduce(wire, y_ring, term, out.at[chunk], first.at[chunk], last.at[chunk])
            total.start()
            sums.append(total)
        for total in sums:
            total.middle()
        hops = []
        for chunk, total in enumerate(sums):
            cross[chunk] = total.finish(0).astype(BF16)
            hops.append((
                wire.send(cross.at[chunk, 0], relay.at[chunk, 0], up_x),
                wire.send(cross.at[chunk, 1], relay.at[chunk, 1], down_x),
            ))
        for chunk, total in enumerate(sums):
            own[chunk] = total.finish(1)
        ends = []
        for chunk, (a, b) in enumerate(hops):
            wire.recv(a, relay.at[chunk, 0])
            c = wire.send(relay.at[chunk, 0], got.at[chunk, 0], up_x)
            wire.recv(b, relay.at[chunk, 1])
            d = wire.send(relay.at[chunk, 1], got.at[chunk, 1], down_x)
            ends.append((c, d))
        for chunk, (c, d) in enumerate(ends):
            wire.recv(c, got.at[chunk, 0])
            wire.recv(d, got.at[chunk, 1])
            yield chunk, [own[chunk, plane] + got[chunk, plane].astype(F32) for plane in range(2)]

    for chunk, update in scatter_columns(
        y_lhs, y_neg, f_buf, u_part, u_out, u_first, u_last, u_own, u_cross, u_relay, u_got
    ):
        blocks = u_part.shape[-1] // BLK
        for plane in range(2):
            for block in range(blocks):
                u_flat[plane, pl.ds(chunk * blocks + block, 16, stride=16), :] = (
                    update[plane][:, block * BLK:(block + 1) * BLK]
                )
    u_send[...] = u_flat[...].astype(BF16).reshape(u_send.shape)

    got = []
    for step in range(1, 8):
        to = row_peer(step)
        got.append(wire.send(u_send.at[to], s4_in.at[row], (to, col)))
    s4_in[pl.ds(row, 1)] = u_send[pl.ds(row, 1)]
    for step in range(1, 8):
        wire.recv(got[step - 1], s4_in.at[lax.rem(row + 8 - step, 8)])
    s4_out[...] = nn_dot(onehot[...], s4_in[...].reshape(512, BLK)).astype(BF16).reshape(s4_out.shape)
    got = []
    for step in range(1, 8):
        to = slot_peer(step)
        got.append(wire.send(s4_out.at[to], rr.at[x_lo, slot, z], (row, to * 2 + core)))
    rr[pl.ds(x_lo, 1), pl.ds(slot, 1), pl.ds(z, 1)] = s4_out[pl.ds(slot, 1)].reshape(1, 1, 1, 48, BLK)
    for step in range(1, 8):
        wire.recv(got[step - 1], rr.at[x_lo, lax.rem(slot + 8 - step, 8), z])

    def rr_piece(x_part):
        return lambda half, place: rr.at[x_part, pl.ds(half * 4, 4), place]

    same = Gather(wire, z_ring, rr_piece(x_lo))
    side = Gather(wire, z_ring, rr_piece(1 - x_lo))
    side0 = wire.send(rr.at[x_lo, pl.ds(0, 4), z], rr.at[x_lo, pl.ds(0, 4), z], side_x)
    side1 = wire.send(rr.at[x_lo, pl.ds(4, 4), z], rr.at[x_lo, pl.ds(4, 4), z], side_x)
    same.start()
    wire.recv(side0, rr.at[1 - x_lo, pl.ds(0, 4), z])
    side.start_half(0)
    wire.recv(side1, rr.at[1 - x_lo, pl.ds(4, 4), z])
    side.start_half(1)
    same.forward()
    side.forward()
    same.finish()
    side.finish()

    wire.recv(rhs_got, rhs_t.at[other])
    for plane in range(2):
        rr_flat[plane] = rr[plane].astype(F32).reshape(rr_flat.shape[1:])
        for block in range(12):
            q, lanes = block // 6, slice((block % 6) * BLK, (block % 6 + 1) * BLK)
            assembled = rr_flat[plane, pl.ds(block, 128, stride=12), :]
            right = (rhs_t[q, plane, :, lanes].astype(F32) - assembled).astype(BF16)
            r_lhs[q, plane * 128:(plane + 1) * 128, lanes] = right
            if plane == 0:
                r_neg[q, 128:256, lanes] = right
            else:
                r_neg[q, 0:128, lanes] = -right
    wire.recv(g_got, g_buf.at[other])
    for chunk, root in scatter_columns(
        r_lhs, r_neg, g_buf, v_part, v_out, v_first, v_last, v_own, v_cross, v_relay, v_got
    ):
        width = v_part.shape[-1]
        for plane in range(2):
            out2_ref[plane, :, chunk * width:(chunk + 1) * width] = root[plane]

    wire.recv(swap_got, y_swap)
    for plane in range(2):
        mine = y_all[plane, pl.ds(z, 1), :, own_cols].reshape(32, 512)
        theirs = y_swap[plane]
        for a in range(2):
            rows16 = slice(a * 16, a * 16 + 16)
            out1_ref[plane, pl.ds(pl.multiple_of((2 * a + core) * 16, 16), 16), :] = mine[rows16]
            out1_ref[plane, pl.ds(pl.multiple_of((2 * a + other) * 16, 16), 16), :] = theirs[rows16]
    wire.drain()


def local(child_rhs, child_inverse_t, boundary_tiles, boundary_lists, root_rhs, root_inverse):
    vmem = pltpu.VMEM
    pivots, own_q = child_inverse_t.shape[1], child_inverse_t.shape[2]
    bounds = boundary_tiles.shape[1]
    root_rows, root_cols = root_inverse.shape[1], root_inverse.shape[2]
    whole = pl.BlockSpec(memory_space=pltpu.VMEM)
    far = pl.BlockSpec(memory_space=pl.ANY)

    def scatter_scratch(width, chunks):
        w = width // chunks
        return [
            vmem((chunks, 2, 2, 4, 16, w), F32),
            vmem((chunks, 6, 2, 16, w), BF16),
            vmem((chunks, 2, 2, 16, w), BF16),
            vmem((chunks, 4, 2, 16, w), BF16),
            vmem((chunks, 2, 16, w), F32),
            vmem((chunks, 2, 16, w), BF16),
            vmem((chunks, 2, 16, w), BF16),
            vmem((chunks, 2, 16, w), BF16),
        ]

    scratch = [
        vmem((2, 2, pivots, own_q), BF16),
        vmem((2, 2, bounds, own_q), BF16),
        vmem((2, 2, root_rows, root_cols), BF16),
        vmem((2, 8, 16, pivots), BF16),
        vmem((256, pivots), BF16),
        vmem((2, 16, pivots), BF16),
        vmem((2, 4, 32, 2 * own_q), F32),
        vmem((6, 32, 2 * own_q), BF16),
        vmem((2, 32, 2 * own_q), BF16),
        vmem((4, 32, 2 * own_q), BF16),
        vmem((2, 4, 32, 2 * own_q), BF16),
        vmem((2, 256, own_q), BF16),
        vmem((2, 256, own_q), BF16),
        vmem((2, 32, own_q), BF16),
        *scatter_scratch(bounds, 2),
        vmem((2, 256, BLK), F32),
        vmem((8, 64, BLK), BF16),
        vmem((8, 64, BLK), BF16),
        vmem((8, 48, BLK), BF16),
        vmem((2, 8, 4, 48, BLK), BF16),
        vmem((2, 1536, BLK), F32),
        vmem((384, 512), BF16),
        vmem((2, 2, 128, root_cols), BF16),
        vmem((2, 128, root_cols), BF16),
        vmem((2, 256, root_cols), BF16),
        vmem((2, 256, root_cols), BF16),
        *scatter_scratch(root_rows, 2),
        pltpu.SemaphoreType.DMA((N_SEMS,)),
        pltpu.SemaphoreType.DMA((N_SEMS,)),
        pltpu.SemaphoreType.DMA((3,)),
    ]
    child_t, root_t = pl.pallas_call(
        kernel,
        out_shape=(
            jax.ShapeDtypeStruct((2, 64, own_q), BF16),
            jax.ShapeDtypeStruct((2, 16, root_rows), F32),
        ),
        in_specs=[whole, far, far, whole, whole, far],
        out_specs=(whole, whole),
        scratch_shapes=scratch,
        compiler_params=pltpu.CompilerParams(
            collective_id=0, has_side_effects=True, vmem_limit_bytes=60 * 1024 * 1024
        ),
    )(
        jnp.transpose(child_rhs, (0, 2, 1)), child_inverse_t, boundary_tiles, boundary_lists, root_rhs, root_inverse
    )
    return jnp.transpose(child_t, (0, 2, 1)), jnp.transpose(root_t, (0, 2, 1))


def solution(mesh):
    return jax.shard_map(
        local,
        mesh=mesh,
        in_specs=(
            P(None, "row", "col"),
            P(None, "row", "col"),
            P(None, "row", "col"),
            P(),
            P(None, "col", None),
            P(None, "row", "col"),
        ),
        out_specs=(P(None, "col", "row"), P(None, "row", "col")),
        check_vma=False,
    )
```

time: 556 us -> 104 us (0.19)
  waiting for transfers between devices: 499 us -> 0 us
  Pallas kernels: 0 us -> 99.2 us
  matrix products: 16.5 us -> 0 us
  between operations: 14 us -> 0.64 us
  local copies, waits for them, and re-layouts: 12.6 us -> 3.18 us
  other arithmetic: 8.4 us -> 0 us
    all_gather x2 -> x0, waiting for transfers between devices: 299 us -> none  [the longest x1 246 us: local(): portion = lax.all_gather(update, ('row', 'col'), axis=0, tiled=True)]
    reduce_scatter x2 -> x0, waiting for transfers between devices: 153 us -> none  [the longest x1 79.6 us: local(): lax.psum_scatter(jnp.stack((real_part, imag_part), axis=1), 'col', scatte...]
    pallas_call x0 -> x1, Pallas kernels: none -> 99.2 us  [local(): pl.pallas_call(kernel, out_shape=(jax.ShapeDtypeStruct((2, 64, own_q), BF...]
    ppermute x2 -> x0, waiting for transfers between devices: 46.5 us -> none  [swapped(): lax.ppermute(x, axis, [(i, i ^ 1 << distance) for i in range(lax.axis_siz...]
    dot_general x13 -> x0, matrix products: 16.5 us -> none  [the longest x8 7.98 us: plain_dot(): return jnp.dot(left, right, preferred_element_type=jnp.float32)]
    unnamed x13 -> x2, local copies, waits for them, and re-layouts: 10.2 us -> 3.18 us
  transfers between devices with their start and end apart: 6 -> 0, of which waited for: 6 -> 0; matrix products, arithmetic and copies ran while one was open for 0% -> 0% of each run, Pallas kernels for 0% -> 0%
where the time goes in v1:
time: 104 us; the launch traced here: 103 us
  Pallas kernels  99.2 us (95%)
  local copies, waits for them, and re-layouts  3.18 us (3%)
    pallas_call x1, Pallas kernels, local(): pl.pallas_call(kernel, out_shape=(jax.ShapeDtypeStruct((2, 64, own_q), BF...  99.2 us
    unnamed x2, local copies, waits for them, and re-layouts  3.18 us

profile of v1, /device:TPU:0, one launch (start us, length us, event | category | flops | bytes accessed | tf_op | source)
XLA Modules:
  0.0 103.0 jit_solution(17192319574520756217)
XLA Ops:
  0.6 99.2 %shard_map.77 = (bf16[2,64,512]{2,1,0:T(8,128)(2,1)}, f32[2,16,1536]{2,1,0:T(8,128)}) custom-call(bf16[2,16,2048]{2,1,0:T(8,128)(2,1)} %bitcast.4, bf16[2,2048,512]{2,1,0:T(8,128)(2,1)} %a_hbm.1, bf16[2,2048,512]{2,1,0:T(8,128)(2,1)} %f_hbm.1, s32[2,64]{1,0:T(2,128)} %lists_ref.1, bf16[2,768,256]{2,1,0:T(8,128)(2,1)} %rhs_ref.1, bf16[2,1536,768]{2,1,0:T(8,128)(2,1)} %g_hbm.1), custom_call_target="tpu_custom_call" | custom-call | tf_op jit(solution)/shard_map/pallas_call | solution.py:461
  99.8 1.6 %copy.10 = bf16[2,512,64]{1,2,0:T(8,128)(2,1)} copy(bf16[2,512,64]{1,2,0:T(8,128)(2,1)} %bitcast.5) | data formatting | bytes 262144
  101.4 1.6 %copy.11 = f32[2,1536,16]{1,2,0:T(8,128)} copy(f32[2,1536,16]{1,2,0:T(8,128)} %bitcast.3) | data formatting | bytes 393216

commit v2 on v1

v2 whole, which is shorter than its diff:
```python
import jax
import jax.numpy as jnp
from jax import lax
from jax.experimental import pallas as pl
from jax.experimental.pallas import tpu as pltpu
from jax.sharding import PartitionSpec as P

MESH = pl.DeviceIdType.MESH
F32 = jnp.float32
BF16 = jnp.bfloat16
N_SEMS = 192
BLK = 128
TILE = 256


class Wire:
    def __init__(self, send_sems, recv_sems, here):
        self.send_sems, self.recv_sems, self.here = send_sems, recv_sems, here
        self.count = 0
        self.started = []

    def send(self, src, dst, device):
        at = self.count
        self.count += 1
        copy = pltpu.make_async_remote_copy(
            src_ref=src, dst_ref=dst, send_sem=self.send_sems.at[at], recv_sem=self.recv_sems.at[at],
            device_id=device, device_id_type=MESH,
        )
        copy.start()
        self.started.append(copy)
        return at

    def recv(self, at, dst):
        pltpu.make_async_remote_copy(
            src_ref=dst, dst_ref=dst, send_sem=self.send_sems.at[at], recv_sem=self.recv_sems.at[at],
            device_id=self.here, device_id_type=MESH,
        ).wait_recv()

    def drain(self):
        for copy in self.started:
            copy.wait_send()


class Ring:
    def __init__(self, me, up_device, down_device):
        self.me = me
        self.up, self.down, self.far = lax.rem(me + 1, 4), lax.rem(me + 3, 4), lax.rem(me + 2, 4)
        self.up_device, self.down_device = up_device, down_device


class Gather:
    def __init__(self, wire, ring, piece, source=None):
        self.wire, self.ring, self.piece = wire, ring, piece
        self.source = source or (lambda half: piece(half, ring.me))

    def start_half(self, half):
        w, r, piece = self.wire, self.ring, self.piece
        src = self.source(half)
        ahead, behind = (r.up_device, r.down_device) if half == 0 else (r.down_device, r.up_device)
        a = w.send(src, piece(half, r.me), ahead)
        b = w.send(src, piece(half, r.me), behind)
        if half == 0:
            self.a0, self.b0 = a, b
        else:
            self.a1, self.b1 = a, b

    def start(self):
        self.start_half(0)
        self.start_half(1)

    def forward(self):
        w, r, piece = self.wire, self.ring, self.piece
        w.recv(self.a0, piece(0, r.down))
        self.f0 = w.send(piece(0, r.down), piece(0, r.down), r.up_device)
        w.recv(self.a1, piece(1, r.up))
        self.f1 = w.send(piece(1, r.up), piece(1, r.up), r.down_device)

    def finish(self):
        w, r, piece = self.wire, self.ring, self.piece
        w.recv(self.b0, piece(0, r.up))
        w.recv(self.b1, piece(1, r.down))
        w.recv(self.f0, piece(0, r.far))
        w.recv(self.f1, piece(1, r.far))


class Reduce:
    def __init__(self, wire, ring, part, out, first, last):
        self.wire, self.ring, self.part, self.out, self.first, self.last = wire, ring, part, out, first, last

    def start(self):
        w, r, out = self.wire, self.ring, self.out
        out[0] = self.part(0, r.far).astype(BF16)
        self.i0 = w.send(out.at[0], self.first.at[0], r.up_device)
        out[1] = self.part(1, r.far).astype(BF16)
        self.i1 = w.send(out.at[1], self.first.at[1], r.down_device)
        out[2] = self.part(1, r.up).astype(BF16)
        self.i2 = w.send(out.at[2], self.last.at[0], r.up_device)
        out[3] = self.part(0, r.down).astype(BF16)
        self.i3 = w.send(out.at[3], self.last.at[1], r.down_device)

    def middle(self):
        w, r, out = self.wire, self.ring, self.out
        w.recv(self.i0, self.first.at[0])
        out[4] = (self.part(0, r.up) + self.first[0].astype(F32)).astype(BF16)
        self.i4 = w.send(out.at[4], self.last.at[2], r.up_device)
        w.recv(self.i1, self.first.at[1])
        out[5] = (self.part(1, r.down) + self.first[1].astype(F32)).astype(BF16)
        self.i5 = w.send(out.at[5], self.last.at[3], r.down_device)

    def finish(self, half):
        w, r, last = self.wire, self.ring, self.last
        if half == 0:
            w.recv(self.i3, last.at[1])
            w.recv(self.i4, last.at[2])
            return self.part(0, r.me) + last[1].astype(F32) + last[2].astype(F32)
        w.recv(self.i2, last.at[0])
        w.recv(self.i5, last.at[3])
        return self.part(1, r.me) + last[0].astype(F32) + last[3].astype(F32)


def nt_dot(left, right):
    return lax.dot_general(left, right, (((1,), (1,)), ((), ())), preferred_element_type=F32)


def nn_dot(left, right):
    return jnp.dot(left, right, preferred_element_type=F32)


def iota(shape, axis):
    return lax.broadcasted_iota(jnp.int32, shape, axis).astype(F32)


def split_by(value, size):
    quotient = jnp.floor((value + 0.5) * (1.0 / size))
    return quotient, value - quotient * size


def kernel(
    b_hbm, a_hbm, f_hbm, lists_hbm, rhs_hbm, g_hbm, out1_ref, out2_ref,
    a_buf, f_buf, g_buf, b_all, b_neg,
    y_part, y_out, y_first, y_last, y_all, y_neg, y_swap,
    u_part, u_out, u_first, u_last, u_flat, u_send,
    s4_in, s4_out, rr, rr_flat, onehot, lists_ref, rhs_ref, rhs_t, rhs_send, r_lhs, r_neg,
    v_part, v_out, v_first, v_last, v_own, v_cross, v_got,
    send_sems, recv_sems, local_sems, token_sem,
):
    row, col = lax.axis_index("row"), lax.axis_index("col")
    x_lo, z = lax.div(row, 4), lax.rem(row, 4)
    slot, core = lax.div(col, 2), lax.rem(col, 2)
    x_hi, y = lax.div(slot, 4), lax.rem(slot, 4)
    x = x_hi * 2 + x_lo
    other = 1 - core

    def device(x, y, z, core):
        return (lax.rem(x, 2) * 4 + z, lax.div(x, 2) * 8 + y * 2 + core)

    def place_of(row, slot):
        return (row, slot * 2 + core)

    across = place_of(row, lax.rem(slot + 4, 8))
    side = place_of(lax.rem(row + 4, 8), slot)
    partner = (row, slot * 2 + other)
    y_ring = Ring(y, device(x, lax.rem(y + 1, 4), z, core), device(x, lax.rem(y + 3, 4), z, core))
    z_ring = Ring(z, device(x, y, lax.rem(z + 1, 4), core), device(x, y, lax.rem(z + 3, 4), core))

    barrier = pltpu.get_barrier_semaphore()
    greet = [y_ring.up_device, y_ring.down_device, across, partner, z_ring.up_device, z_ring.down_device, side]
    for peer in greet:
        pl.semaphore_signal(barrier, inc=1, device_id=peer, device_id_type=MESH)

    chunks1, width1 = b_all.shape[0], b_all.shape[4]

    def b_source(chunk, plane):
        return b_hbm.at[plane, :, pl.ds(chunk * width1, width1)]

    fetch = []

    def get(src, dst):
        copy = pltpu.make_async_copy(src, dst, local_sems.at[len(fetch)])
        copy.start()
        fetch.append(copy)
        return copy

    own_b = [
        get(b_source(chunk, plane), b_all.at[chunk, plane, slot]) for chunk in range(chunks1) for plane in range(2)
    ]
    own_lists = get(lists_hbm, lists_ref)
    own_rhs = get(rhs_hbm, rhs_ref)
    own_a = get(a_hbm, a_buf.at[core])
    pl.semaphore_wait(barrier, len(greet))

    wire = Wire(send_sems, recv_sems, (row, col))

    def b_piece(chunk, x_half):
        return lambda half, place: b_all.at[chunk, half, x_half * 4 + place]

    near, away, crossed = [], [], []
    for chunk in range(chunks1):
        crossed.append([
            wire.send(b_source(chunk, plane), b_all.at[chunk, plane, slot], across) for plane in range(2)
        ])
        near.append(Gather(
            wire, y_ring, b_piece(chunk, x_hi), source=lambda half, chunk=chunk: b_source(chunk, half)
        ))
        near[chunk].start()
        away.append(Gather(wire, y_ring, b_piece(chunk, 1 - x_hi)))
    a_got = wire.send(a_hbm, a_buf.at[core], partner)

    own_lists.wait()
    own_rhs.wait()
    cols = onehot.shape[2]
    blocks = u_part.shape[-1] // BLK
    t_block, t_rest = split_by(iota((384, cols), 0), 48)
    t_q, t_rest = split_by(t_rest, 24)
    t_col, t_at = split_by(t_rest, 6)
    s_chip, s_rest = split_by(iota((384, cols), 1), 4 * blocks)
    s_col, _ = split_by(s_rest, blocks)
    e_chip, e_rest = split_by(iota((64, cols), 1), 4 * blocks)
    _, e_at = split_by(e_rest, blocks)
    _, e_z = split_by(e_chip, 4)
    list_values = lists_ref[...].astype(F32).astype(BF16)
    for chunk in range(onehot.shape[0]):
        spread = (e_z * 16 + (chunk * blocks) + e_at == iota((64, cols), 0)).astype(BF16)
        spread_lists = nn_dot(list_values, spread)
        source_list = jnp.where(iota((1, cols), 1) < cols // 2, spread_lists[0:1], spread_lists[1:2])
        onehot[chunk] = jnp.where(
            (t_col == s_col) & (source_list == t_block * 12 + t_q * 6 + t_at), 1.0, 0.0
        ).astype(BF16)

    pick_slot, pick_rest = split_by(iota((128, 256), 0), 16)
    for mine in (False, True):
        parity = (core if mine else other).astype(F32)
        pick = (pick_slot * 32 + parity * 16 + pick_rest == iota((128, 256), 1)).astype(BF16)
        for plane in range(2):
            turned = nt_dot(pick, rhs_ref[plane]).astype(BF16)
            if mine:
                rhs_t[pl.ds(core, 1), plane] = turned[None]
            else:
                rhs_send[plane] = turned

    for chunk in range(chunks1):
        for plane in range(2):
            wire.recv(crossed[chunk][plane], b_all.at[chunk, plane, (1 - x_hi) * 4 + y])
            away[chunk].start_half(plane)
        near[chunk].forward()
    for chunk in range(chunks1):
        away[chunk].forward()
    own_a.wait()
    own_f = get(f_hbm, f_buf.at[core])
    wire.recv(a_got, a_buf.at[other])
    f_got = wire.send(f_hbm, f_buf.at[core], partner)
    rhs_got = wire.send(rhs_send, rhs_t.at[core], partner)

    per_q = a_buf.shape[3] // TILE

    def s1_multiply(chunk, q):
        rows = pl.ds(chunk * width1, width1)

        def tile_step(tile, carry):
            lanes = pl.ds(pl.multiple_of(tile * TILE, TILE), TILE)
            value = nn_dot(b_all[chunk].reshape(256, width1), a_buf[q, 0, rows, lanes])
            value += nn_dot(b_neg[...], a_buf[q, 1, rows, lanes])
            value = value.reshape(2, 4, 32, TILE)
            if chunk > 0:
                value += y_part[q, :, :, :, lanes]
            y_part[q, :, :, :, lanes] = value
            return carry

        lax.fori_loop(0, per_q, tile_step, 0)

    y_sums, y_gathers = [], []
    for q in range(2):
        y_sums.append(Reduce(
            wire, z_ring, lambda half, place, q=q: y_part[q, half, place], y_out.at[q], y_first.at[q], y_last.at[q]
        ))
        y_gathers.append(Gather(wire, z_ring, lambda half, place, q=q: y_all.at[q, half, place]))

    for chunk in range(chunks1):
        near[chunk].finish()
        away[chunk].finish()
        for plane in range(2):
            own_b[chunk * 2 + plane].wait()
        b_neg[0:128] = -b_all[chunk, 1].reshape(128, width1)
        b_neg[128:256] = b_all[chunk, 0].reshape(128, width1)
        for q in range(2):
            s1_multiply(chunk, q)
            if chunk == chunks1 - 1:
                y_sums[q].start()

    for q in range(2):
        y_sums[q].middle()
    for q in range(2):
        for half in range(2):
            y_all[q, half, pl.ds(z, 1)] = y_sums[q].finish(half).astype(BF16)[None]
            y_gathers[q].start_half(half)
    for q in range(2):
        y_gathers[q].forward()
    own_f.wait()
    own_g = get(g_hbm, g_buf.at[core])
    wire.recv(f_got, f_buf.at[other])
    g_got = wire.send(g_hbm, g_buf.at[core], partner)

    def multiply(lhs, neg, weights, q, part, chunk):
        width = part.shape[-1]

        def tile_step(at, carry):
            src = pl.ds(pl.multiple_of(chunk * width + at * TILE, TILE), TILE)
            value = nt_dot(lhs(q), weights[q, 0, src, :])
            value += nt_dot(neg[q], weights[q, 1, src, :])
            value = value.reshape(2, 2, 4, 16, TILE)
            where = pl.ds(pl.multiple_of(at * TILE, TILE), TILE)
            if q > 0:
                value += part[chunk, :, :, :, :, where]
            part[chunk, :, :, :, :, where] = value
            return carry

        lax.fori_loop(0, width // TILE, tile_step, 0)

    def y_reduce(part, out, first, last, chunk):
        def term(half, place):
            return part[chunk, :, (x_hi if half == 1 else 1 - x_hi), place]

        return Reduce(wire, y_ring, term, out.at[chunk], first.at[chunk], last.at[chunk])

    chunks3 = u_part.shape[0]

    def y_lhs(q):
        return y_all[q].reshape(256, y_all.shape[-1])

    u_sums = []
    for q in range(2):
        y_gathers[q].finish()
        if q == 1:
            swap_got = wire.send(y_all.at[other, :, z], y_swap, partner)
        y_neg[q, 0:128] = -y_all[q, 1].reshape(128, y_all.shape[-1])
        y_neg[q, 128:256] = y_all[q, 0].reshape(128, y_all.shape[-1])
        for chunk in range(chunks3):
            multiply(y_lhs, y_neg, f_buf, q, u_part, chunk)
            if q == 1:
                u_sums.append(y_reduce(u_part, u_out, u_first, u_last, chunk))
                u_sums[chunk].start()
    pl.semaphore_signal(token_sem, inc=1, device_id=side, device_id_type=MESH)
    for chunk in range(chunks3):
        u_sums[chunk].middle()

    def s4_peer(half, step):
        return lax.rem(row + step, 8), (slot if half == 1 else lax.rem(slot + 4, 8))

    s4_got = []
    for chunk in range(chunks3):
        for half in range(2):
            update = u_sums[chunk].finish(half)
            for plane in range(2):
                for block in range(blocks):
                    u_flat[plane, pl.ds(block, 16, stride=blocks), :] = update[plane][:, block * BLK:(block + 1) * BLK]
            u_send[chunk, half] = u_flat[...].astype(BF16).reshape(u_send.shape[2:])
            if chunk == 0 and half == 0:
                pl.semaphore_wait(token_sem, 1)
            for step in range(half, 8):
                to_row, to_slot = s4_peer(half, step)
                s4_got.append((chunk, half, step, wire.send(
                    u_send.at[chunk, half, to_row], s4_in.at[chunk, x_hi, row], place_of(to_row, to_slot)
                )))
        s4_in[chunk, pl.ds(x_hi, 1), pl.ds(row, 1)] = u_send[chunk, 1:2, pl.ds(row, 1)]
    for chunk, half, step, at in s4_got:
        wire.recv(at, s4_in.at[chunk, (x_hi if half == 1 else 1 - x_hi), lax.rem(row + 8 - step, 8)])
    total = None
    for chunk in range(chunks3):
        for half in range(2):
            term = nn_dot(onehot[chunk], s4_in[chunk, half].reshape(cols, BLK))
            total = term if total is None else total + term
    s4_out[...] = total.astype(BF16).reshape(s4_out.shape)
    s4_got = []
    for turn in (1, 0):
        to_row = lax.rem(row + 4 * turn, 8)
        for step in range(1 - turn, 8):
            to = lax.rem(slot + step, 8)
            s4_got.append((turn, step, wire.send(s4_out.at[to], rr.at[:, x_lo, slot, z], place_of(to_row, to))))
    rr[:, pl.ds(x_lo, 1), pl.ds(slot, 1), pl.ds(z, 1)] = s4_out[pl.ds(slot, 1)].reshape(2, 1, 1, 1, 24, BLK)
    for turn, step, at in s4_got:
        wire.recv(at, rr.at[:, (1 - x_lo if turn == 1 else x_lo), lax.rem(slot + 8 - step, 8), z])

    r_gathers = [
        Gather(wire, z_ring, lambda half, place, q=q: rr.at[q, half, :, place]) for q in range(2)
    ]
    for q in range(2):
        r_gathers[q].start()
    for q in range(2):
        r_gathers[q].forward()
    own_g.wait()

    def root_lhs(q):
        return r_lhs[q]

    v_sums = []
    chunks5 = v_part.shape[0]
    for q in range(2):
        r_gathers[q].finish()
        if q == 0:
            wire.recv(rhs_got, rhs_t.at[other])
            wire.recv(g_got, g_buf.at[other])
        for plane in range(2):
            rr_flat[...] = rr[q, plane].astype(F32).reshape(rr_flat.shape)
            for block in range(6):
                lanes = slice(block * BLK, (block + 1) * BLK)
                assembled = rr_flat[pl.ds(block, 128, stride=6), :]
                right = (rhs_t[q, plane, :, lanes].astype(F32) - assembled).astype(BF16)
                r_lhs[q, plane * 128:(plane + 1) * 128, lanes] = right
                if plane == 0:
                    r_neg[q, 128:256, lanes] = right
                else:
                    r_neg[q, 0:128, lanes] = -right
        for chunk in range(chunks5):
            multiply(root_lhs, r_neg, g_buf, q, v_part, chunk)
            if q == 1:
                v_sums.append(y_reduce(v_part, v_out, v_first, v_last, chunk))
                v_sums[chunk].start()
    for chunk in range(chunks5):
        v_sums[chunk].middle()
    v_hops = []
    for chunk in range(chunks5):
        v_cross[chunk] = v_sums[chunk].finish(0).astype(BF16)
        v_hops.append(wire.send(v_cross.at[chunk], v_got.at[chunk], across))
    for chunk in range(chunks5):
        v_own[chunk] = v_sums[chunk].finish(1)

    wire.recv(swap_got, y_swap)
    for plane in range(2):
        mine = y_all[pl.ds(core, 1), plane, pl.ds(z, 1)].reshape(32, y_all.shape[-1])
        theirs = y_swap[plane]
        for a in range(2):
            rows16 = slice(a * 16, a * 16 + 16)
            out1_ref[plane, pl.ds(pl.multiple_of((2 * a + core) * 16, 16), 16), :] = mine[rows16]
            out1_ref[plane, pl.ds(pl.multiple_of((2 * a + other) * 16, 16), 16), :] = theirs[rows16]
    width5 = v_part.shape[-1]
    for chunk in range(chunks5):
        wire.recv(v_hops[chunk], v_got.at[chunk])
        out2_ref[:, :, chunk * width5:(chunk + 1) * width5] = v_own[chunk] + v_got[chunk].astype(F32)
    wire.drain()


def copy_out(in1_ref, in2_ref, out1_ref, out2_ref):
    out1_ref[...] = in1_ref[...]
    out2_ref[...] = in2_ref[...]


def local(child_rhs, child_inverse_t, boundary_tiles, boundary_lists, root_rhs, root_inverse):
    vmem = pltpu.VMEM
    pivots, own_q = child_inverse_t.shape[1], child_inverse_t.shape[2]
    bounds = boundary_tiles.shape[1]
    root_rows, root_cols = root_inverse.shape[1], root_inverse.shape[2]
    whole = pl.BlockSpec(memory_space=pltpu.VMEM)
    far = pl.BlockSpec(memory_space=pl.ANY)

    def scatter_scratch(width, chunks):
        w = width // chunks
        return [
            vmem((chunks, 2, 2, 4, 16, w), F32),
            vmem((chunks, 6, 2, 16, w), BF16),
            vmem((chunks, 2, 2, 16, w), BF16),
            vmem((chunks, 4, 2, 16, w), BF16),
        ]

    chunks1, chunks3, chunks5 = 2, 2, 2
    blocks3 = bounds // chunks3 // BLK
    w5 = root_rows // chunks5
    scratch = [
        vmem((2, 2, pivots, own_q), BF16),
        vmem((2, 2, bounds, own_q), BF16),
        vmem((2, 2, root_rows, root_cols), BF16),
        vmem((chunks1, 2, 8, 16, pivots // chunks1), BF16),
        vmem((256, pivots // chunks1), BF16),
        vmem((2, 2, 4, 32, own_q), F32),
        vmem((2, 6, 32, own_q), BF16),
        vmem((2, 2, 32, own_q), BF16),
        vmem((2, 4, 32, own_q), BF16),
        vmem((2, 2, 4, 32, own_q), BF16),
        vmem((2, 256, own_q), BF16),
        vmem((2, 32, own_q), BF16),
        *scatter_scratch(bounds, chunks3),
        vmem((2, 16 * blocks3, BLK), F32),
        vmem((chunks3, 2, 8, 4 * blocks3, BLK), BF16),
        vmem((chunks3, 2, 8, 4 * blocks3, BLK), BF16),
        vmem((8, 2, 24, BLK), BF16),
        vmem((2, 2, 8, 4, 24, BLK), BF16),
        vmem((768, BLK), F32),
        vmem((chunks3, 384, 32 * blocks3), BF16),
        vmem((2, 64), jnp.int32),
        vmem((2, root_cols, 256), BF16),
        vmem((2, 2, 128, root_cols), BF16),
        vmem((2, 128, root_cols), BF16),
        vmem((2, 256, root_cols), BF16),
        vmem((2, 256, root_cols), BF16),
        *scatter_scratch(root_rows, chunks5),
        vmem((chunks5, 2, 16, w5), F32),
        vmem((chunks5, 2, 16, w5), BF16),
        vmem((chunks5, 2, 16, w5), BF16),
        pltpu.SemaphoreType.DMA((N_SEMS,)),
        pltpu.SemaphoreType.DMA((N_SEMS,)),
        pltpu.SemaphoreType.DMA((12,)),
        pltpu.SemaphoreType.REGULAR,
    ]
    shapes = (
        jax.ShapeDtypeStruct((2, 64, own_q), BF16),
        jax.ShapeDtypeStruct((2, 16, root_rows), F32),
    )
    parts = pl.pallas_call(
        kernel,
        out_shape=shapes,
        in_specs=[far] * 6,
        out_specs=(whole, whole),
        scratch_shapes=scratch,
        compiler_params=pltpu.CompilerParams(
            collective_id=0, has_side_effects=True, vmem_limit_bytes=60 * 1024 * 1024
        ),
    )(
        jnp.transpose(child_rhs, (0, 2, 1)), child_inverse_t, boundary_tiles, boundary_lists, root_rhs, root_inverse
    )
    child_t, root_t = pl.pallas_call(
        copy_out, out_shape=shapes, in_specs=[whole, whole], out_specs=(whole, whole),
    )(*parts)
    return jnp.transpose(child_t, (0, 2, 1)), jnp.transpose(root_t, (0, 2, 1))


def solution(mesh):
    return jax.shard_map(
        local,
        mesh=mesh,
        in_specs=(
            P(None, "row", "col"),
            P(None, "row", "col"),
            P(None, "row", "col"),
            P(),
            P(None, "col", None),
            P(None, "row", "col"),
        ),
        out_specs=(P(None, "col", "row"), P(None, "row", "col")),
        check_vma=False,
    )
```

time: 104 us -> 87 us (0.84)
  Pallas kernels: 99.2 us -> 85.7 us
  local copies, waits for them, and re-layouts: 3.18 us -> 0 us
    pallas_call x1 -> x2, Pallas kernels: 99.2 us -> 85.7 us  [the longest x1 84 us: local(): pl.pallas_call(kernel, out_shape=shapes, in_specs=[far] * 6, out_specs=(w...]
    unnamed x2 -> x0, local copies, waits for them, and re-layouts: 3.18 us -> none
where the time goes in v2:
time: 87 us; the launch traced here: 86.3 us
  Pallas kernels  85.7 us (99%)
    pallas_call x1, Pallas kernels, local(): pl.pallas_call(kernel, out_shape=shapes, in_specs=[far] * 6, out_specs=(w...  84 us

profile of v2, /device:TPU:0, one launch (start us, length us, event | category | flops | bytes accessed | tf_op | source)
XLA Modules:
  0.0 86.3 jit_solution(1316002562689001238)
XLA Ops:
  0.6 84.0 %shard_map.77 = (bf16[2,64,512]{2,1,0:T(8,128)(2,1)}, f32[2,16,1536]{2,1,0:T(8,128)}) custom-call(bf16[2,16,2048]{2,1,0:T(8,128)(2,1)} %bitcast.3, bf16[2,2048,512]{2,1,0:T(8,128)(2,1)} %a_hbm.1, bf16[2,2048,512]{2,1,0:T(8,128)(2,1)} %f_hbm.1, s32[2,64]{1,0:T(2,128)} %lists_hbm.1, bf16[2,768,256]{2,1,0:T(8,128)(2,1)} %rhs_hbm.1, bf16[2,1536,768]{2,1,0:T(8,128)(2,1)} %g_hbm.1), custom_call_target="tpu_custom_call" | custom-call | tf_op jit(solution)/shard_map/pallas_call | solution.py:507
  84.6 1.7 %shard_map.78 = (bf16[2,64,512]{2,1,0:T(8,128)(2,1)}, f32[2,16,1536]{2,1,0:T(8,128)}) custom-call(bf16[2,64,512]{2,1,0:T(8,128)(2,1)} %get-tuple-element.6.in1_ref, f32[2,16,1536]{2,1,0:T(8,128)} %get-tuple-element.7.in2_ref), custom_call_target="tpu_custom_call" | custom-call | tf_op jit(solution)/shard_map/pallas_call | solution.py:519

commit v3 on v2

v3 whole, which is shorter than its diff:
```python
import jax
import jax.numpy as jnp
from jax import lax
from jax.experimental import pallas as pl
from jax.experimental.pallas import tpu as pltpu
from jax.sharding import PartitionSpec as P

MESH = pl.DeviceIdType.MESH
F32 = jnp.float32
BF16 = jnp.bfloat16
N_SENDS, N_RECVS = 96, 121
CROSS, NEAR = 4, 2
BLK = 128
TILE = 256


class Wire:
    def __init__(self, send_sems, recv_sems, group_sends, group_recvs, here):
        self.send_sems, self.recv_sems, self.here = send_sems, recv_sems, here
        self.group_sends, self.group_recvs = group_sends, group_recvs
        self.count = self.high = 0
        self.free = []
        self.started = []

    def copy(self, src, dst, send_sem, recv_sem, device):
        return pltpu.make_async_remote_copy(
            src_ref=src, dst_ref=dst, send_sem=send_sem, recv_sem=recv_sem, device_id=device, device_id_type=MESH
        )

    def send(self, src, dst, device):
        at = self.count
        self.count += 1
        if self.free:
            slot = self.free.pop()
        else:
            slot = self.high
            self.high += 1
        copy = self.copy(src, dst, self.send_sems.at[slot], self.recv_sems.at[at], device)
        copy.start()
        self.started.append((slot, copy))
        return at

    def block(self, many):
        at, slot = self.count, self.high
        self.count += many
        self.high += many
        return at, slot

    def send_block(self, block, step, src, dst, device):
        self.copy(src, dst, self.send_sems.at[block[1] + step], self.recv_sems.at[block[0] + step], device).start()

    def sent_block(self, block, step, src, dst, device):
        at = block[1] + step
        self.started.append(
            (at, self.copy(src, dst, self.send_sems.at[at], self.recv_sems.at[block[0] + step], device))
        )

    def recv(self, at, dst):
        self.copy(dst, dst, self.send_sems.at[0], self.recv_sems.at[at], self.here).wait_recv()

    def recycle(self, keep=0):
        done = self.started[:len(self.started) - keep]
        self.started = self.started[len(done):]
        for slot, copy in done:
            copy.wait_send()
            self.free.append(slot)

    def send_in(self, group, src, dst, device):
        self.copy(src, dst, self.group_sends.at[group], self.group_recvs.at[group], device).start()

    def keep_in(self, group, src, dst):
        pltpu.make_async_copy(src, dst, self.group_recvs.at[group]).start()

    def recv_all(self, group, dst):
        self.copy(dst, dst, self.group_sends.at[group], self.group_recvs.at[group], self.here).wait_recv()

    def sent_all(self, group, src):
        self.copy(src, src, self.group_sends.at[group], self.group_recvs.at[group], self.here).wait_send()


class Ring:
    def __init__(self, me, up_device, down_device, far_device):
        self.me = me
        self.up, self.down, self.far = lax.rem(me + 1, 4), lax.rem(me + 3, 4), lax.rem(me + 2, 4)
        self.up_device, self.down_device, self.far_device = up_device, down_device, far_device


class Gather:
    def __init__(self, wire, ring, piece, source=None):
        self.wire, self.ring, self.piece = wire, ring, piece
        self.source = source or (lambda half: piece(half, ring.me))

    def start_half(self, half):
        w, r, piece = self.wire, self.ring, self.piece
        src = self.source(half)
        ahead, behind = (r.up_device, r.down_device) if half == 0 else (r.down_device, r.up_device)
        a = w.send(src, piece(half, r.me), ahead)
        b = w.send(src, piece(half, r.me), behind)
        if half == 0:
            self.a0, self.b0 = a, b
        else:
            self.a1, self.b1 = a, b

    def start(self):
        self.start_half(0)
        self.start_half(1)

    def forward(self):
        w, r, piece = self.wire, self.ring, self.piece
        w.recv(self.a0, piece(0, r.down))
        self.f0 = w.send(piece(0, r.down), piece(0, r.down), r.up_device)
        w.recv(self.a1, piece(1, r.up))
        self.f1 = w.send(piece(1, r.up), piece(1, r.up), r.down_device)

    def finish(self):
        w, r, piece = self.wire, self.ring, self.piece
        w.recv(self.b0, piece(0, r.up))
        w.recv(self.b1, piece(1, r.down))
        w.recv(self.f0, piece(0, r.far))
        w.recv(self.f1, piece(1, r.far))


class Reduce:
    def __init__(self, wire, ring, chunks, part, out, first, last):
        self.wire, self.ring, self.chunks, self.part = wire, ring, chunks, part
        self.out, self.first, self.last = out, first, last
        self.blocks = [wire.block(chunks) for _ in range(4)]
        self.late = {}

    def early(self, chunk):
        r, out, first, last = self.ring, self.out, self.first, self.last
        return (
            (0, r.far, out.at[chunk, 0], first.at[chunk, 0], r.up_device),
            (1, r.far, out.at[chunk, 1], first.at[chunk, 1], r.down_device),
            (1, r.up, out.at[chunk, 2], last.at[chunk, 0], r.up_device),
            (0, r.down, out.at[chunk, 3], last.at[chunk, 1], r.down_device),
        )

    def start(self, chunk):
        for block, (half, place, src, dst, device) in zip(self.blocks, self.early(chunk)):
            src[...] = self.part(chunk, half, place).astype(BF16)
            self.wire.send_block(block, chunk, src, dst, device)

    def started(self):
        for chunk in range(self.chunks):
            for block, (_, _, src, dst, device) in zip(self.blocks, self.early(chunk)):
                self.wire.sent_block(block, chunk, src, dst, device)

    def middle(self, chunk):
        w, r, out, first, last = self.wire, self.ring, self.out, self.first, self.last
        late = []
        for half, place, device in ((0, r.up, r.up_device), (1, r.down, r.down_device)):
            w.recv(self.blocks[half][0] + chunk, first.at[chunk, half])
            out[chunk, 4 + half] = (self.part(chunk, half, place) + first[chunk, half].astype(F32)).astype(BF16)
            late.append(w.send(out.at[chunk, 4 + half], last.at[chunk, 2 + half], device))
        self.late[chunk] = late

    def finish(self, chunk, half):
        w, last = self.wire, self.last
        w.recv(self.blocks[3 - half][0] + chunk, last.at[chunk, 1 - half])
        w.recv(self.late[chunk][half], last.at[chunk, 2 + half])
        return self.part(chunk, half, self.ring.me) + last[chunk, 1 - half].astype(F32) + last[chunk, 2 + half].astype(F32)


class DirectGather:
    def __init__(self, wire, ring, whole):
        self.wire, self.ring, self.whole = wire, ring, whole

    def start(self):
        w, r, whole = self.wire, self.ring, self.whole
        self.at = [w.send(whole(r.me), whole(r.me), to) for to in (r.far_device, r.up_device, r.down_device)]

    def finish(self):
        r = self.ring
        for at, place in zip(self.at, (r.far, r.down, r.up)):
            self.wire.recv(at, self.whole(place))


class DirectReduce:
    def __init__(self, wire, ring, chunks, part, out, last):
        self.wire, self.ring, self.chunks, self.part = wire, ring, chunks, part
        self.out, self.last = out, last
        self.blocks = [wire.block(chunks) for _ in range(3)]

    def copies(self, chunk):
        r = self.ring
        for at, (place, device) in enumerate(((r.far, r.far_device), (r.up, r.up_device), (r.down, r.down_device))):
            yield at, place, self.out.at[chunk, at], self.last.at[chunk, at], device

    def start(self, chunk):
        for at, place, src, dst, device in self.copies(chunk):
            for half in range(2):
                src[half] = self.part(chunk, half, place).astype(BF16)
            self.wire.send_block(self.blocks[at], chunk, src, dst, device)

    def started(self):
        for chunk in range(self.chunks):
            for at, _, src, dst, device in self.copies(chunk):
                self.wire.sent_block(self.blocks[at], chunk, src, dst, device)

    def middle(self, chunk):
        pass

    def finish(self, chunk, half):
        if half == 0:
            for at in range(3):
                self.wire.recv(self.blocks[at][0] + chunk, self.last.at[chunk, at])
        value = self.part(chunk, half, self.ring.me)
        for at in range(3):
            value = value + self.last[chunk, at, half].astype(F32)
        return value


def nt_dot(left, right):
    return lax.dot_general(left, right, (((1,), (1,)), ((), ())), preferred_element_type=F32)


def nn_dot(left, right):
    return jnp.dot(left, right, preferred_element_type=F32)


def iota(shape, axis):
    return lax.broadcasted_iota(jnp.int32, shape, axis).astype(F32)


def split_by(value, size):
    quotient = jnp.floor((value + 0.5) * (1.0 / size))
    return quotient, value - quotient * size


def kernel(
    b_hbm, a_hbm, f_hbm, lists_hbm, rhs_hbm, g_hbm, out1_ref, out2_ref,
    a_buf, f_buf, g_buf, b_all, b_neg,
    y_part, y_out, y_last, y_all, y_lhs, y_neg, y_swap,
    u_part, u_out, u_first, u_last, u_flat, u_send,
    s4_in, s4_out, rr, rr_flat, onehot, lists_ref, rhs_ref, rhs_t, rhs_send, r_lhs, r_neg,
    v_part, v_out, v_first, v_last, v_own, v_cross, v_got,
    send_sems, recv_sems, group_sends, group_recvs, local_sems, token_sem,
):
    row, col = lax.axis_index("row"), lax.axis_index("col")
    x_lo, z = lax.div(row, 4), lax.rem(row, 4)
    slot, core = lax.div(col, 2), lax.rem(col, 2)
    x_hi, y = lax.div(slot, 4), lax.rem(slot, 4)
    x = x_hi * 2 + x_lo
    other = 1 - core

    def device(x, y, z, core):
        return (lax.rem(x, 2) * 4 + z, lax.div(x, 2) * 8 + y * 2 + core)

    def place_of(row, slot):
        return (row, slot * 2 + core)

    across = place_of(row, lax.rem(slot + 4, 8))
    side = place_of(lax.rem(row + 4, 8), slot)
    partner = (row, slot * 2 + other)
    y_ring = Ring(
        y, device(x, lax.rem(y + 1, 4), z, core), device(x, lax.rem(y + 3, 4), z, core),
        device(x, lax.rem(y + 2, 4), z, core),
    )
    z_ring = Ring(
        z, device(x, y, lax.rem(z + 1, 4), core), device(x, y, lax.rem(z + 3, 4), core),
        device(x, y, lax.rem(z + 2, 4), core),
    )

    barrier = pltpu.get_barrier_semaphore()
    greet = [
        y_ring.up_device, y_ring.down_device, across, partner,
        z_ring.up_device, z_ring.down_device, z_ring.far_device, side,
    ]
    for peer in greet:
        pl.semaphore_signal(barrier, inc=1, device_id=peer, device_id_type=MESH)

    pivots = b_hbm.shape[2]

    def lanes_of(chunk, chunks):
        return pl.ds(chunk * (pivots // chunks), pivots // chunks)

    fetch = []

    def get(src, dst):
        copy = pltpu.make_async_copy(src, dst, local_sems.at[len(fetch)])
        copy.start()
        fetch.append(copy)
        return copy

    own_b = get(b_hbm, b_all.at[:, slot])
    own_lists = get(lists_hbm, lists_ref)
    own_rhs = get(rhs_hbm, rhs_ref)
    own_a = get(a_hbm, a_buf.at[core])
    pl.semaphore_wait(barrier, len(greet))

    wire = Wire(send_sems, recv_sems, group_sends, group_recvs, (row, col))

    def b_piece(chunk, chunks, x_half):
        return lambda half, place: b_all.at[half, x_half * 4 + place, :, lanes_of(chunk, chunks)]

    near, away, crossed = [], [], []
    for chunk in range(CROSS):
        crossed.append(wire.send(
            b_hbm.at[:, :, lanes_of(chunk, CROSS)], b_all.at[:, slot, :, lanes_of(chunk, CROSS)], across
        ))
        away.append(Gather(wire, y_ring, b_piece(chunk, CROSS, 1 - x_hi)))
    for chunk in range(NEAR):
        near.append(Gather(
            wire, y_ring, b_piece(chunk, NEAR, x_hi),
            source=lambda half, chunk=chunk: b_hbm.at[half, :, lanes_of(chunk, NEAR)],
        ))
        near[chunk].start()
    a_got = [wire.send(a_hbm.at[plane], a_buf.at[core, plane], partner) for plane in range(2)]

    own_lists.wait()
    own_rhs.wait()
    cols = onehot.shape[2]
    blocks = u_send.shape[2] // 4
    t_block, t_rest = split_by(iota((384, cols), 0), 48)
    t_q, t_rest = split_by(t_rest, 24)
    t_col, t_at = split_by(t_rest, 6)
    s_chip, s_rest = split_by(iota((384, cols), 1), 4 * blocks)
    s_col, _ = split_by(s_rest, blocks)
    e_chip, e_rest = split_by(iota((64, cols), 1), 4 * blocks)
    _, e_at = split_by(e_rest, blocks)
    _, e_z = split_by(e_chip, 4)
    list_values = lists_ref[...].astype(F32).astype(BF16)
    for chunk in range(onehot.shape[0]):
        spread = (e_z * 16 + (chunk * blocks) + e_at == iota((64, cols), 0)).astype(BF16)
        spread_lists = nn_dot(list_values, spread)
        source_list = jnp.where(iota((1, cols), 1) < cols // 2, spread_lists[0:1], spread_lists[1:2])
        onehot[chunk] = jnp.where(
            (t_col == s_col) & (source_list == t_block * 12 + t_q * 6 + t_at), 1.0, 0.0
        ).astype(BF16)

    pick_slot, pick_rest = split_by(iota((128, 256), 0), 16)
    for mine in (False, True):
        parity = (core if mine else other).astype(F32)
        pick = (pick_slot * 32 + parity * 16 + pick_rest == iota((128, 256), 1)).astype(BF16)
        for plane in range(2):
            turned = nt_dot(pick, rhs_ref[plane]).astype(BF16)
            if mine:
                rhs_t[pl.ds(core, 1), plane] = turned[None]
            else:
                rhs_send[plane] = turned

    for chunk in range(CROSS):
        wire.recv(crossed[chunk], b_all.at[:, (1 - x_hi) * 4 + y, :, lanes_of(chunk, CROSS)])
        away[chunk].start()
        if chunk * NEAR % CROSS == 0:
            near[chunk * NEAR // CROSS].forward()
    for chunk in range(CROSS):
        away[chunk].forward()
    own_a.wait()
    own_f = get(f_hbm, f_buf.at[core])
    for plane in range(2):
        wire.recv(a_got[plane], a_buf.at[other, plane])
    f_got = wire.send(f_hbm, f_buf.at[core], partner)
    rhs_got = wire.send(rhs_send, rhs_t.at[core], partner)
    for gather in near + away:
        gather.finish()
    own_b.wait()

    b_neg[0:128] = -b_all[1].reshape(128, pivots)
    b_neg[128:256] = b_all[0].reshape(128, pivots)
    chunks2, width2 = y_part.shape[0], y_part.shape[-1]
    per_q = chunks2 // 2
    y_sums = DirectReduce(wire, z_ring, chunks2, lambda chunk, half, place: y_part[chunk, half, place], y_out, y_last)
    y_gathers = [
        DirectGather(wire, z_ring, lambda place, chunk=chunk: y_all.at[chunk, :, place]) for chunk in range(chunks2)
    ]

    def s1_step(chunk, carry):
        q = lax.div(chunk, per_q)
        lanes = pl.ds(pl.multiple_of(lax.rem(chunk, per_q) * width2, width2), width2)
        value = nn_dot(b_all[...].reshape(256, pivots), a_buf[q, 0, :, lanes])
        value += nn_dot(b_neg[...], a_buf[q, 1, :, lanes])
        y_part[pl.ds(chunk, 1)] = value.reshape(1, 2, 4, 32, width2)
        y_sums.start(chunk)
        return carry

    lax.fori_loop(0, chunks2, s1_step, 0)
    y_sums.started()

    for chunk in range(chunks2):
        for half in range(2):
            y_all[chunk, half, pl.ds(z, 1)] = y_sums.finish(chunk, half).astype(BF16)[None]
        y_gathers[chunk].start()
    own_f.wait()
    own_g = get(g_hbm, g_buf.at[core])
    wire.recv(f_got, f_buf.at[other])
    wire.recycle(keep=3 * chunks2)
    g_got = wire.send(g_hbm, g_buf.at[core], partner)
    for chunk in range(chunks2):
        y_gathers[chunk].finish()
        q, lanes = chunk // per_q, slice(chunk % per_q * width2, (chunk % per_q + 1) * width2)
        real, imag = y_all[chunk, 0].reshape(128, width2), y_all[chunk, 1].reshape(128, width2)
        y_lhs[q, 0:128, lanes] = real
        y_lhs[q, 128:256, lanes] = imag
        y_neg[q, 0:128, lanes] = -imag
        y_neg[q, 128:256, lanes] = real
    swap_got = wire.send(y_all.at[pl.ds(other * per_q, per_q), :, z], y_swap, partner)

    def multiply(lhs, neg, weights, part, out, first, last):
        chunks, width = part.shape[0], part.shape[-1]

        def term(chunk, half, place):
            return part[chunk, :, (x_hi if half == 1 else 1 - x_hi), place]

        sums = Reduce(wire, y_ring, chunks, term, out, first, last)

        def step(chunk, carry):
            def tile_step(at, carry):
                src = pl.ds(pl.multiple_of(chunk * width + at * TILE, TILE), TILE)
                value = None
                for q in range(2):
                    for left, plane in ((lhs, 0), (neg, 1)):
                        product = nt_dot(left[q], weights[q, plane, src, :])
                        value = product if value is None else value + product
                where = pl.ds(pl.multiple_of(at * TILE, TILE), TILE)
                part[pl.ds(chunk, 1), :, :, :, :, where] = value.reshape(1, 2, 2, 4, 16, TILE)
                return carry

            lax.fori_loop(0, width // TILE, tile_step, 0)
            sums.start(chunk)
            return carry

        lax.fori_loop(0, chunks, step, 0)
        sums.started()
        return sums

    chunks3 = u_part.shape[0]
    u_sums = multiply(y_lhs, y_neg, f_buf, u_part, u_out, u_first, u_last)
    pl.semaphore_signal(token_sem, inc=1, device_id=side, device_id_type=MESH)
    for chunk in range(chunks3):
        u_sums.middle(chunk)

    def s4_peer(half, step):
        return lax.rem(row + step, 8), (slot if half == 1 else lax.rem(slot + 4, 8))

    groups = u_send.shape[0]
    per_group = chunks3 // groups
    width_blocks = blocks // per_group
    for group in range(groups):
        for half in range(2):
            for part in range(per_group):
                update = u_sums.finish(group * per_group + part, half)
                for plane in range(2):
                    for block in range(width_blocks):
                        u_flat[plane, pl.ds(part * width_blocks + block, 16, stride=blocks), :] = (
                            update[plane][:, block * BLK:(block + 1) * BLK]
                        )
            u_send[group, half * 8:half * 8 + 8] = u_flat[...].astype(BF16).reshape(8, 4 * blocks, BLK)
            if group == 0 and half == 0:
                pl.semaphore_wait(token_sem, 1)
            for step in range(half, 8):
                to_row, to_slot = s4_peer(half, step)
                wire.send_in(
                    group, u_send.at[group, half * 8 + to_row], s4_in.at[group, x_hi, row], place_of(to_row, to_slot)
                )
        wire.keep_in(group, u_send.at[group, 8 + row], s4_in.at[group, x_hi, row])
    for group in range(groups):
        wire.recv_all(group, s4_in.at[group])
    total = None
    for group in range(groups):
        for half in range(2):
            term = nn_dot(onehot[group], s4_in[group, half].reshape(cols, BLK))
            total = term if total is None else total + term
    packed = total.astype(BF16).reshape(8, 2, 24, BLK)
    s4_out[0:8] = packed
    s4_out[8:16] = packed
    for turn in (1, 0):
        to_row = lax.rem(row + 4 * turn, 8)
        for step in range(1 - turn, 8):
            to = lax.rem(slot + step, 8)
            wire.send_in(groups, s4_out.at[turn * 8 + to], rr.at[:, x_lo, slot, z], place_of(to_row, to))
    wire.keep_in(groups, s4_out.at[slot], rr.at[:, x_lo, slot, z])
    wire.recv_all(groups, rr.at[:, :, :, z])

    r_gathers = [
        DirectGather(wire, z_ring, lambda place, q=q: rr.at[q, :, :, place]) for q in range(2)
    ]
    for q in range(2):
        r_gathers[q].start()
    own_g.wait()

    chunks5 = v_part.shape[0]
    wire.recv(rhs_got, rhs_t.at[other])
    wire.recv(g_got, g_buf.at[other])
    for q in range(2):
        r_gathers[q].finish()
        for plane in range(2):
            rr_flat[...] = rr[q, plane].astype(F32).reshape(rr_flat.shape)
            for block in range(6):
                lanes = slice(block * BLK, (block + 1) * BLK)
                assembled = rr_flat[pl.ds(block, 128, stride=6), :]
                right = (rhs_t[q, plane, :, lanes].astype(F32) - assembled).astype(BF16)
                r_lhs[q, plane * 128:(plane + 1) * 128, lanes] = right
                if plane == 0:
                    r_neg[q, 128:256, lanes] = right
                else:
                    r_neg[q, 0:128, lanes] = -right
    v_sums = multiply(r_lhs, r_neg, g_buf, v_part, v_out, v_first, v_last)
    for chunk in range(chunks5):
        v_sums.middle(chunk)
    v_hops = []
    for chunk in range(chunks5):
        v_cross[chunk] = v_sums.finish(chunk, 0).astype(BF16)
        v_hops.append(wire.send(v_cross.at[chunk], v_got.at[chunk], across))
    for chunk in range(chunks5):
        v_own[chunk] = v_sums.finish(chunk, 1)

    wire.recv(swap_got, y_swap)
    for at in range(per_q):
        lanes = slice(at * width2, (at + 1) * width2)
        for plane in range(2):
            mine = y_all[pl.ds(core * per_q + at, 1), plane, pl.ds(z, 1)].reshape(32, width2)
            theirs = y_swap[at, plane]
            for a in range(2):
                rows16 = slice(a * 16, a * 16 + 16)
                out1_ref[plane, pl.ds(pl.multiple_of((2 * a + core) * 16, 16), 16), lanes] = mine[rows16]
                out1_ref[plane, pl.ds(pl.multiple_of((2 * a + other) * 16, 16), 16), lanes] = theirs[rows16]
    width5 = v_part.shape[-1]
    for chunk in range(chunks5):
        wire.recv(v_hops[chunk], v_got.at[chunk])
        out2_ref[:, :, chunk * width5:(chunk + 1) * width5] = v_own[chunk] + v_got[chunk].astype(F32)
    wire.recycle()
    for group in range(groups):
        wire.sent_all(group, u_send.at[group, 0:15])
    wire.sent_all(groups, s4_out.at[0:15])


def copy_out(in1_ref, in2_ref, out1_ref, out2_ref):
    out1_ref[...] = in1_ref[...]
    out2_ref[...] = in2_ref[...]


def local(child_rhs, child_inverse_t, boundary_tiles, boundary_lists, root_rhs, root_inverse):
    vmem = pltpu.VMEM
    pivots, own_q = child_inverse_t.shape[1], child_inverse_t.shape[2]
    bounds = boundary_tiles.shape[1]
    root_rows, root_cols = root_inverse.shape[1], root_inverse.shape[2]
    whole = pl.BlockSpec(memory_space=pltpu.VMEM)
    far = pl.BlockSpec(memory_space=pl.ANY)

    def scatter_scratch(width, chunks):
        w = width // chunks
        return [
            vmem((chunks, 2, 2, 4, 16, w), F32),
            vmem((chunks, 6, 2, 16, w), BF16),
            vmem((chunks, 2, 2, 16, w), BF16),
            vmem((chunks, 4, 2, 16, w), BF16),
        ]

    chunks2, chunks3, chunks5, groups = 4, 4, 3, 2
    w2 = 2 * own_q // chunks2
    blocks = bounds // groups // BLK
    w5 = root_rows // chunks5
    scratch = [
        vmem((2, 2, pivots, own_q), BF16),
        vmem((2, 2, bounds, own_q), BF16),
        vmem((2, 2, root_rows, root_cols), BF16),
        vmem((2, 8, 16, pivots), BF16),
        vmem((256, pivots), BF16),
        vmem((chunks2, 2, 4, 32, w2), F32),
        vmem((chunks2, 3, 2, 32, w2), BF16),
        vmem((chunks2, 3, 2, 32, w2), BF16),
        vmem((chunks2, 2, 4, 32, w2), BF16),
        vmem((2, 256, own_q), BF16),
        vmem((2, 256, own_q), BF16),
        vmem((chunks2 // 2, 2, 32, w2), BF16),
        *scatter_scratch(bounds, chunks3),
        vmem((2, 16 * blocks, BLK), F32),
        vmem((groups, 16, 4 * blocks, BLK), BF16),
        vmem((groups, 2, 8, 4 * blocks, BLK), BF16),
        vmem((16, 2, 24, BLK), BF16),
        vmem((2, 2, 8, 4, 24, BLK), BF16),
        vmem((768, BLK), F32),
        vmem((groups, 384, 32 * blocks), BF16),
        vmem((2, 64), jnp.int32),
        vmem((2, root_cols, 256), BF16),
        vmem((2, 2, 128, root_cols), BF16),
        vmem((2, 128, root_cols), BF16),
        vmem((2, 256, root_cols), BF16),
        vmem((2, 256, root_cols), BF16),
        *scatter_scratch(root_rows, chunks5),
        vmem((chunks5, 2, 16, w5), F32),
        vmem((chunks5, 2, 16, w5), BF16),
        vmem((chunks5, 2, 16, w5), BF16),
        pltpu.SemaphoreType.DMA((N_SENDS,)),
        pltpu.SemaphoreType.DMA((N_RECVS,)),
        pltpu.SemaphoreType.DMA((groups + 1,)),
        pltpu.SemaphoreType.DMA((groups + 1,)),
        pltpu.SemaphoreType.DMA((6,)),
        pltpu.SemaphoreType.REGULAR,
    ]
    shapes = (
        jax.ShapeDtypeStruct((2, 64, own_q), BF16),
        jax.ShapeDtypeStruct((2, 16, root_rows), F32),
    )
    parts = pl.pallas_call(
        kernel,
        out_shape=shapes,
        in_specs=[far] * 6,
        out_specs=(whole, whole),
        scratch_shapes=scratch,
        compiler_params=pltpu.CompilerParams(
            collective_id=0, has_side_effects=True, vmem_limit_bytes=60 * 1024 * 1024
        ),
    )(
        jnp.transpose(child_rhs, (0, 2, 1)), child_inverse_t, boundary_tiles, boundary_lists, root_rhs, root_inverse
    )
    child_t, root_t = pl.pallas_call(
        copy_out, out_shape=shapes, in_specs=[whole, whole], out_specs=(whole, whole),
    )(*parts)
    return jnp.transpose(child_t, (0, 2, 1)), jnp.transpose(root_t, (0, 2, 1))


def solution(mesh):
    return jax.shard_map(
        local,
        mesh=mesh,
        in_specs=(
            P(None, "row", "col"),
            P(None, "row", "col"),
            P(None, "row", "col"),
            P(),
            P(None, "col", None),
            P(None, "row", "col"),
        ),
        out_specs=(P(None, "col", "row"), P(None, "row", "col")),
        check_vma=False,
    )
```

time: 87 us -> 80.5 us (0.925)
  Pallas kernels: 85.7 us -> 79.2 us
    pallas_call x1, Pallas kernels: 84 us -> 77.5 us  [local(): pl.pallas_call(kernel, out_shape=shapes, in_specs=[far] * 6, out_specs=(w...]
where the time goes in v3:
time: 80.5 us; the launch traced here: 79.9 us
  Pallas kernels  79.2 us (98%)
    pallas_call x1, Pallas kernels, local(): pl.pallas_call(kernel, out_shape=shapes, in_specs=[far] * 6, out_specs=(w...  77.5 us
    pallas_call x1, Pallas kernels, local(): pl.pallas_call(copy_out, out_shape=shapes, in_specs=[whole, whole], out_s...  1.72 us

profile of v3, /device:TPU:0, one launch (start us, length us, event | category | flops | bytes accessed | tf_op | source)
XLA Modules:
  0.0 79.9 jit_solution(12128867427401150161)
XLA Ops:
  0.6 77.5 %shard_map.77 = (bf16[2,64,512]{2,1,0:T(8,128)(2,1)}, f32[2,16,1536]{2,1,0:T(8,128)}) custom-call(bf16[2,16,2048]{2,1,0:T(8,128)(2,1)} %bitcast.3, bf16[2,2048,512]{2,1,0:T(8,128)(2,1)} %a_hbm.1, bf16[2,2048,512]{2,1,0:T(8,128)(2,1)} %f_hbm.1, s32[2,64]{1,0:T(2,128)} %lists_hbm.1, bf16[2,768,256]{2,1,0:T(8,128)(2,1)} %rhs_hbm.1, bf16[2,1536,768]{2,1,0:T(8,128)(2,1)} %g_hbm.1), custom_call_target="tpu_custom_call" | custom-call | tf_op jit(solution)/shard_map/pallas_call | solution.py:597
  78.2 1.7 %shard_map.78 = (bf16[2,64,512]{2,1,0:T(8,128)(2,1)}, f32[2,16,1536]{2,1,0:T(8,128)}) custom-call(bf16[2,64,512]{2,1,0:T(8,128)(2,1)} %get-tuple-element.6.in1_ref, f32[2,16,1536]{2,1,0:T(8,128)} %get-tuple-element.7.in2_ref), custom_call_target="tpu_custom_call" | custom-call | tf_op jit(solution)/shard_map/pallas_call | solution.py:609

commit v4 on v3

--- a/solution.py
+++ b/solution.py
@@ -8,7 +8,7 @@
 MESH = pl.DeviceIdType.MESH
 F32 = jnp.float32
 BF16 = jnp.bfloat16
-N_SENDS, N_RECVS = 96, 121
+N_SENDS, N_RECVS = 65, 121
 CROSS, NEAR = 4, 2
 BLK = 128
 TILE = 256
@@ -41,8 +41,13 @@
         return at
 
     def block(self, many):
-        at, slot = self.count, self.high
+        at, free = self.count, sorted(self.free)
         self.count += many
+        for i in range(len(free) - many + 1):
+            if free[i + many - 1] - free[i] == many - 1:
+                self.free = free[:i] + free[i + many:]
+                return at, free[i]
+        slot = self.high
         self.high += many
         return at, slot
 
@@ -286,8 +291,8 @@
     own_b = get(b_hbm, b_all.at[:, slot])
     own_lists = get(lists_hbm, lists_ref)
     own_rhs = get(rhs_hbm, rhs_ref)
-    own_a = get(a_hbm, a_buf.at[core])
     pl.semaphore_wait(barrier, len(greet))
+    own_b.wait()
 
     wire = Wire(send_sems, recv_sems, group_sends, group_recvs, (row, col))
 
@@ -297,15 +302,15 @@
     near, away, crossed = [], [], []
     for chunk in range(CROSS):
         crossed.append(wire.send(
-            b_hbm.at[:, :, lanes_of(chunk, CROSS)], b_all.at[:, slot, :, lanes_of(chunk, CROSS)], across
+            b_all.at[:, slot, :, lanes_of(chunk, CROSS)], b_all.at[:, slot, :, lanes_of(chunk, CROSS)], across
         ))
         away.append(Gather(wire, y_ring, b_piece(chunk, CROSS, 1 - x_hi)))
     for chunk in range(NEAR):
         near.append(Gather(
             wire, y_ring, b_piece(chunk, NEAR, x_hi),
-            source=lambda half, chunk=chunk: b_hbm.at[half, :, lanes_of(chunk, NEAR)],
         ))
         near[chunk].start()
+    own_a = get(a_hbm, a_buf.at[core])
     a_got = [wire.send(a_hbm.at[plane], a_buf.at[core, plane], partner) for plane in range(2)]
 
     own_lists.wait()
@@ -340,11 +345,12 @@
             else:
                 rhs_send[plane] = turned
 
+    near[0].forward()
     for chunk in range(CROSS):
         wire.recv(crossed[chunk], b_all.at[:, (1 - x_hi) * 4 + y, :, lanes_of(chunk, CROSS)])
         away[chunk].start()
-        if chunk * NEAR % CROSS == 0:
-            near[chunk * NEAR // CROSS].forward()
+        if chunk + 1 < NEAR:
+            near[chunk + 1].forward()
     for chunk in range(CROSS):
         away[chunk].forward()
     own_a.wait()
@@ -355,7 +361,7 @@
     rhs_got = wire.send(rhs_send, rhs_t.at[core], partner)
     for gather in near + away:
         gather.finish()
-    own_b.wait()
+    wire.recycle(keep=2)
 
     b_neg[0:128] = -b_all[1].reshape(128, pivots)
     b_neg[128:256] = b_all[0].reshape(128, pivots)
@@ -431,9 +437,10 @@
     for chunk in range(chunks3):
         u_sums.middle(chunk)
 
-    def s4_peer(half, step):
-        return lax.rem(row + step, 8), (slot if half == 1 else lax.rem(slot + 4, 8))
-
+    def s4_row(x_step, z_step):
+        return lax.rem(x_lo + x_step, 2) * 4 + lax.rem(z + z_step, 4)
+
+    far_first = (2, 1, 3, 0)
     groups = u_send.shape[0]
     per_group = chunks3 // groups
     width_blocks = blocks // per_group
@@ -449,11 +456,15 @@
             u_send[group, half * 8:half * 8 + 8] = u_flat[...].astype(BF16).reshape(8, 4 * blocks, BLK)
             if group == 0 and half == 0:
                 pl.semaphore_wait(token_sem, 1)
-            for step in range(half, 8):
-                to_row, to_slot = s4_peer(half, step)
-                wire.send_in(
-                    group, u_send.at[group, half * 8 + to_row], s4_in.at[group, x_hi, row], place_of(to_row, to_slot)
-                )
+            to_slot = slot if half == 1 else lax.rem(slot + 4, 8)
+            for z_step in far_first:
+                for x_step in ((1, 0) if half == 1 else (0, 1)):
+                    if half == 1 and x_step == 0 and z_step == 0:
+                        continue
+                    to_row = s4_row(x_step, z_step)
+                    wire.send_in(
+                        group, u_send.at[group, half * 8 + to_row], s4_in.at[group, x_hi, row], place_of(to_row, to_slot)
+                    )
         wire.keep_in(group, u_send.at[group, 8 + row], s4_in.at[group, x_hi, row])
     for group in range(groups):
         wire.recv_all(group, s4_in.at[group])
@@ -465,11 +476,14 @@
     packed = total.astype(BF16).reshape(8, 2, 24, BLK)
     s4_out[0:8] = packed
     s4_out[8:16] = packed
-    for turn in (1, 0):
-        to_row = lax.rem(row + 4 * turn, 8)
-        for step in range(1 - turn, 8):
-            to = lax.rem(slot + step, 8)
-            wire.send_in(groups, s4_out.at[turn * 8 + to], rr.at[:, x_lo, slot, z], place_of(to_row, to))
+    for y_step in far_first:
+        for half_step, x_step in ((1, 0), (1, 1), (0, 1), (0, 0)):
+            if half_step == 0 and x_step == 0 and y_step == 0:
+                continue
+            to = (x_hi if half_step == 0 else 1 - x_hi) * 4 + lax.rem(y + y_step, 4)
+            wire.send_in(
+                groups, s4_out.at[x_step * 8 + to], rr.at[:, x_lo, slot, z], place_of(s4_row(x_step, 0), to)
+            )
     wire.keep_in(groups, s4_out.at[slot], rr.at[:, x_lo, slot, z])
     wire.recv_all(groups, rr.at[:, :, :, z])
 
@@ -524,11 +538,6 @@
     for group in range(groups):
         wire.sent_all(group, u_send.at[group, 0:15])
     wire.sent_all(groups, s4_out.at[0:15])
-
-
-def copy_out(in1_ref, in2_ref, out1_ref, out2_ref):
-    out1_ref[...] = in1_ref[...]
-    out2_ref[...] = in2_ref[...]
 
 
 def local(child_rhs, child_inverse_t, boundary_tiles, boundary_lists, root_rhs, root_inverse):
@@ -591,10 +600,10 @@
         pltpu.SemaphoreType.REGULAR,
     ]
     shapes = (
-        jax.ShapeDtypeStruct((2, 64, own_q), BF16),
-        jax.ShapeDtypeStruct((2, 16, root_rows), F32),
+        vmem((2, 64, own_q), BF16),
+        vmem((2, 16, root_rows), F32),
     )
-    parts = pl.pallas_call(
+    child_t, root_t = pl.pallas_call(
         kernel,
         out_shape=shapes,
         in_specs=[far] * 6,
@@ -606,9 +615,6 @@
     )(
         jnp.transpose(child_rhs, (0, 2, 1)), child_inverse_t, boundary_tiles, boundary_lists, root_rhs, root_inverse
     )
-    child_t, root_t = pl.pallas_call(
-        copy_out, out_shape=shapes, in_specs=[whole, whole], out_specs=(whole, whole),
-    )(*parts)
     return jnp.transpose(child_t, (0, 2, 1)), jnp.transpose(root_t, (0, 2, 1))
 
 

time: 80.5 us -> 78 us (0.969)
  Pallas kernels: 79.2 us -> 75.9 us
  local copies, waits for them, and re-layouts: 0 us -> 1.33 us
    pallas_call x1 -> x0, Pallas kernels: 1.72 us -> none  [local(): pl.pallas_call(copy_out, out_shape=shapes, in_specs=[whole, whole], out_s...]
    pallas_call x1, Pallas kernels: 77.5 us -> 75.9 us  [local(): pl.pallas_call(kernel, out_shape=shapes, in_specs=[far] * 6, out_specs=(w...]
    unnamed x0 -> x2, local copies, waits for them, and re-layouts: none -> 1.33 us
where the time goes in v4:
time: 78 us; the launch traced here: 77.9 us
  Pallas kernels  75.9 us (97%)
  local copies, waits for them, and re-layouts  1.33 us (2%)
    pallas_call x1, Pallas kernels, local(): pl.pallas_call(kernel, out_shape=shapes, in_specs=[far] * 6, out_specs=(w...  75.9 us

profile of v4, /device:TPU:0, one launch (start us, length us, event | category | flops | bytes accessed | tf_op | source)
XLA Modules:
  0.0 77.9 jit_solution(5822198341328468901)
XLA Ops:
  0.6 75.9 %shard_map.77 = (bf16[2,64,512]{2,1,0:T(8,128)(2,1)S(1)}, f32[2,16,1536]{2,1,0:T(8,128)S(1)}) custom-call(bf16[2,16,2048]{2,1,0:T(8,128)(2,1)} %bitcast.5, bf16[2,2048,512]{2,1,0:T(8,128)(2,1)} %a_hbm.1, bf16[2,2048,512]{2,1,0:T(8,128)(2,1)} %f_hbm.1, s32[2,64]{1,0:T(2,128)} %lists_hbm.1, bf16[2,768,256]{2,1,0:T(8,128)(2,1)} %rhs_hbm.1, ...), custom_call_target="tpu_custom_call" | custom-call | tf_op jit(solution)/shard_map/pallas_call | solution.py:606
  76.6 0.7 copy.10
  77.2 0.7 copy.11

commit v5 on v4

--- a/solution.py
+++ b/solution.py
@@ -8,7 +8,8 @@
 MESH = pl.DeviceIdType.MESH
 F32 = jnp.float32
 BF16 = jnp.bfloat16
-N_SENDS, N_RECVS = 65, 121
+N_SENDS, N_RECVS = 55, 100
+SPLIT3, SPLIT5 = 3, 2
 CROSS, NEAR = 4, 2
 BLK = 128
 TILE = 256
@@ -185,7 +186,7 @@
     def __init__(self, wire, ring, chunks, part, out, last):
         self.wire, self.ring, self.chunks, self.part = wire, ring, chunks, part
         self.out, self.last = out, last
-        self.blocks = [wire.block(chunks) for _ in range(3)]
+        self.block = wire.block(chunks)
 
     def copies(self, chunk):
         r = self.ring
@@ -196,26 +197,38 @@
         for at, place, src, dst, device in self.copies(chunk):
             for half in range(2):
                 src[half] = self.part(chunk, half, place).astype(BF16)
-            self.wire.send_block(self.blocks[at], chunk, src, dst, device)
+            self.wire.send_block(self.block, chunk, src, dst, device)
 
     def started(self):
         for chunk in range(self.chunks):
-            for at, _, src, dst, device in self.copies(chunk):
-                self.wire.sent_block(self.blocks[at], chunk, src, dst, device)
+            self.wire.sent_block(self.block, chunk, self.out.at[chunk], self.last.at[chunk], self.wire.here)
 
     def middle(self, chunk):
         pass
 
     def finish(self, chunk, half):
         if half == 0:
-            for at in range(3):
-                self.wire.recv(self.blocks[at][0] + chunk, self.last.at[chunk, at])
+            self.wire.recv(self.block[0] + chunk, self.last.at[chunk])
         value = self.part(chunk, half, self.ring.me)
         for at in range(3):
             value = value + self.last[chunk, at, half].astype(F32)
         return value
 
 
+class Mixed:
+    def __init__(self, relayed, direct, split):
+        self.relayed, self.direct, self.split = relayed, direct, split
+
+    def middle(self, chunk):
+        if chunk < self.split:
+            self.relayed.middle(chunk)
+
+    def finish(self, chunk, half):
+        if chunk < self.split:
+            return self.relayed.finish(chunk, half)
+        return self.direct.finish(chunk - self.split, half)
+
+
 def nt_dot(left, right):
     return lax.dot_general(left, right, (((1,), (1,)), ((), ())), preferred_element_type=F32)
 
@@ -237,9 +250,9 @@
     b_hbm, a_hbm, f_hbm, lists_hbm, rhs_hbm, g_hbm, out1_ref, out2_ref,
     a_buf, f_buf, g_buf, b_all, b_neg,
     y_part, y_out, y_last, y_all, y_lhs, y_neg, y_swap,
-    u_part, u_out, u_first, u_last, u_flat, u_send,
+    u_part, u_out, u_first, u_last, u_dout, u_dlast, u_flat, u_send,
     s4_in, s4_out, rr, rr_flat, onehot, lists_ref, rhs_ref, rhs_t, rhs_send, r_lhs, r_neg,
-    v_part, v_out, v_first, v_last, v_own, v_cross, v_got,
+    v_part, v_out, v_first, v_last, v_dout, v_dlast, v_own, v_cross, v_got,
     send_sems, recv_sems, group_sends, group_recvs, local_sems, token_sem,
 ):
     row, col = lax.axis_index("row"), lax.axis_index("col")
@@ -304,7 +317,12 @@
         crossed.append(wire.send(
             b_all.at[:, slot, :, lanes_of(chunk, CROSS)], b_all.at[:, slot, :, lanes_of(chunk, CROSS)], across
         ))
-        away.append(Gather(wire, y_ring, b_piece(chunk, CROSS, 1 - x_hi)))
+        if chunk < CROSS - 1:
+            away.append(Gather(wire, y_ring, b_piece(chunk, CROSS, 1 - x_hi)))
+        else:
+            away.append(DirectGather(
+                wire, y_ring, lambda place, chunk=chunk: b_all.at[:, (1 - x_hi) * 4 + place, :, lanes_of(chunk, CROSS)]
+            ))
     for chunk in range(NEAR):
         near.append(Gather(
             wire, y_ring, b_piece(chunk, NEAR, x_hi),
@@ -351,7 +369,7 @@
         away[chunk].start()
         if chunk + 1 < NEAR:
             near[chunk + 1].forward()
-    for chunk in range(CROSS):
+    for chunk in range(CROSS - 1):
         away[chunk].forward()
     own_a.wait()
     own_f = get(f_hbm, f_buf.at[core])
@@ -403,15 +421,19 @@
         y_neg[q, 128:256, lanes] = real
     swap_got = wire.send(y_all.at[pl.ds(other * per_q, per_q), :, z], y_swap, partner)
 
-    def multiply(lhs, neg, weights, part, out, first, last):
-        chunks, width = part.shape[0], part.shape[-1]
+    def multiply(lhs, neg, weights, part, out, first, last, direct_out, direct_last):
+        chunks, width, split = part.shape[0], part.shape[-1], out.shape[0]
 
         def term(chunk, half, place):
             return part[chunk, :, (x_hi if half == 1 else 1 - x_hi), place]
 
-        sums = Reduce(wire, y_ring, chunks, term, out, first, last)
-
-        def step(chunk, carry):
+        relayed = Reduce(wire, y_ring, split, term, out, first, last)
+        direct = DirectReduce(
+            wire, y_ring, chunks - split, lambda chunk, half, place: term(chunk + split, half, place),
+            direct_out, direct_last,
+        )
+
+        def product(chunk):
             def tile_step(at, carry):
                 src = pl.ds(pl.multiple_of(chunk * width + at * TILE, TILE), TILE)
                 value = None
@@ -424,15 +446,25 @@
                 return carry
 
             lax.fori_loop(0, width // TILE, tile_step, 0)
-            sums.start(chunk)
+
+        def relayed_step(chunk, carry):
+            product(chunk)
+            relayed.start(chunk)
             return carry
 
-        lax.fori_loop(0, chunks, step, 0)
-        sums.started()
-        return sums
+        def direct_step(chunk, carry):
+            product(chunk + split)
+            direct.start(chunk)
+            return carry
+
+        lax.fori_loop(0, split, relayed_step, 0)
+        lax.fori_loop(0, chunks - split, direct_step, 0)
+        relayed.started()
+        direct.started()
+        return Mixed(relayed, direct, split)
 
     chunks3 = u_part.shape[0]
-    u_sums = multiply(y_lhs, y_neg, f_buf, u_part, u_out, u_first, u_last)
+    u_sums = multiply(y_lhs, y_neg, f_buf, u_part, u_out, u_first, u_last, u_dout, u_dlast)
     pl.semaphore_signal(token_sem, inc=1, device_id=side, device_id_type=MESH)
     for chunk in range(chunks3):
         u_sums.middle(chunk)
@@ -510,7 +542,7 @@
                     r_neg[q, 128:256, lanes] = right
                 else:
                     r_neg[q, 0:128, lanes] = -right
-    v_sums = multiply(r_lhs, r_neg, g_buf, v_part, v_out, v_first, v_last)
+    v_sums = multiply(r_lhs, r_neg, g_buf, v_part, v_out, v_first, v_last, v_dout, v_dlast)
     for chunk in range(chunks5):
         v_sums.middle(chunk)
     v_hops = []
@@ -548,13 +580,15 @@
     whole = pl.BlockSpec(memory_space=pltpu.VMEM)
     far = pl.BlockSpec(memory_space=pl.ANY)
 
-    def scatter_scratch(width, chunks):
+    def scatter_scratch(width, chunks, split):
         w = width // chunks
         return [
             vmem((chunks, 2, 2, 4, 16, w), F32),
-            vmem((chunks, 6, 2, 16, w), BF16),
-            vmem((chunks, 2, 2, 16, w), BF16),
-            vmem((chunks, 4, 2, 16, w), BF16),
+            vmem((split, 6, 2, 16, w), BF16),
+            vmem((split, 2, 2, 16, w), BF16),
+            vmem((split, 4, 2, 16, w), BF16),
+            vmem((chunks - split, 3, 2, 2, 16, w), BF16),
+            vmem((chunks - split, 3, 2, 2, 16, w), BF16),
         ]
 
     chunks2, chunks3, chunks5, groups = 4, 4, 3, 2
@@ -574,7 +608,7 @@
         vmem((2, 256, own_q), BF16),
         vmem((2, 256, own_q), BF16),
         vmem((chunks2 // 2, 2, 32, w2), BF16),
-        *scatter_scratch(bounds, chunks3),
+        *scatter_scratch(bounds, chunks3, SPLIT3),
         vmem((2, 16 * blocks, BLK), F32),
         vmem((groups, 16, 4 * blocks, BLK), BF16),
         vmem((groups, 2, 8, 4 * blocks, BLK), BF16),
@@ -588,7 +622,7 @@
         vmem((2, 128, root_cols), BF16),
         vmem((2, 256, root_cols), BF16),
         vmem((2, 256, root_cols), BF16),
-        *scatter_scratch(root_rows, chunks5),
+        *scatter_scratch(root_rows, chunks5, SPLIT5),
         vmem((chunks5, 2, 16, w5), F32),
         vmem((chunks5, 2, 16, w5), BF16),
         vmem((chunks5, 2, 16, w5), BF16),

time: 78 us -> 76.9 us (0.986)
  Pallas kernels: 75.9 us -> 74.8 us
    pallas_call x1, Pallas kernels: 75.9 us -> 74.8 us  [local(): pl.pallas_call(kernel, out_shape=shapes, in_specs=[far] * 6, out_specs=(w...]
where the time goes in v5:
time: 76.9 us; the launch traced here: 76.8 us
  Pallas kernels  74.8 us (97%)
  local copies, waits for them, and re-layouts  1.33 us (2%)
    pallas_call x1, Pallas kernels, local(): pl.pallas_call(kernel, out_shape=shapes, in_specs=[far] * 6, out_specs=(w...  74.8 us

profile of v5, /device:TPU:0, one launch (start us, length us, event | category | flops | bytes accessed | tf_op | source)
XLA Modules:
  0.0 76.8 jit_solution(111964646466381657)
XLA Ops:
  0.6 74.8 %shard_map.77 = (bf16[2,64,512]{2,1,0:T(8,128)(2,1)S(1)}, f32[2,16,1536]{2,1,0:T(8,128)S(1)}) custom-call(bf16[2,16,2048]{2,1,0:T(8,128)(2,1)} %bitcast.5, bf16[2,2048,512]{2,1,0:T(8,128)(2,1)} %a_hbm.1, bf16[2,2048,512]{2,1,0:T(8,128)(2,1)} %f_hbm.1, s32[2,64]{1,0:T(2,128)} %lists_hbm.1, bf16[2,768,256]{2,1,0:T(8,128)(2,1)} %rhs_hbm.1, ...), custom_call_target="tpu_custom_call" | custom-call | tf_op jit(solution)/shard_map/pallas_call | solution.py:640
  75.5 0.7 copy.10
  76.1 0.7 copy.11

commit v6 on v5

--- a/solution.py
+++ b/solution.py
@@ -8,8 +8,8 @@
 MESH = pl.DeviceIdType.MESH
 F32 = jnp.float32
 BF16 = jnp.bfloat16
-N_SENDS, N_RECVS = 55, 100
-SPLIT3, SPLIT5 = 3, 2
+N_SENDS, N_RECVS = 39, 81
+SPLIT3, SPLIT5 = 3, 1
 CROSS, NEAR = 4, 2
 BLK = 128
 TILE = 256
@@ -169,17 +169,18 @@
 
 
 class DirectGather:
-    def __init__(self, wire, ring, whole):
-        self.wire, self.ring, self.whole = wire, ring, whole
+    def __init__(self, wire, ring, whole, three):
+        self.wire, self.ring, self.whole, self.three = wire, ring, whole, three
 
     def start(self):
         w, r, whole = self.wire, self.ring, self.whole
-        self.at = [w.send(whole(r.me), whole(r.me), to) for to in (r.far_device, r.up_device, r.down_device)]
+        self.block = w.block(1)
+        for to in (r.far_device, r.up_device, r.down_device):
+            w.send_block(self.block, 0, whole(r.me), whole(r.me), to)
+        w.sent_block(self.block, 0, self.three(), self.three(), w.here)
 
     def finish(self):
-        r = self.ring
-        for at, place in zip(self.at, (r.far, r.down, r.up)):
-            self.wire.recv(at, self.whole(place))
+        self.wire.recv(self.block[0], self.three())
 
 
 class DirectReduce:
@@ -321,7 +322,8 @@
             away.append(Gather(wire, y_ring, b_piece(chunk, CROSS, 1 - x_hi)))
         else:
             away.append(DirectGather(
-                wire, y_ring, lambda place, chunk=chunk: b_all.at[:, (1 - x_hi) * 4 + place, :, lanes_of(chunk, CROSS)]
+                wire, y_ring, lambda place, chunk=chunk: b_all.at[:, (1 - x_hi) * 4 + place, :, lanes_of(chunk, CROSS)],
+                lambda chunk=chunk: b_all.at[:, pl.ds((1 - x_hi) * 4, 3), :, lanes_of(chunk, CROSS)],
             ))
     for chunk in range(NEAR):
         near.append(Gather(
@@ -387,7 +389,11 @@
     per_q = chunks2 // 2
     y_sums = DirectReduce(wire, z_ring, chunks2, lambda chunk, half, place: y_part[chunk, half, place], y_out, y_last)
     y_gathers = [
-        DirectGather(wire, z_ring, lambda place, chunk=chunk: y_all.at[chunk, :, place]) for chunk in range(chunks2)
+        DirectGather(
+            wire, z_ring, lambda place, chunk=chunk: y_all.at[chunk, :, place],
+            lambda chunk=chunk: y_all.at[chunk, :, pl.ds(0, 3)],
+        )
+        for chunk in range(chunks2)
     ]
 
     def s1_step(chunk, carry):
@@ -409,7 +415,7 @@
     own_f.wait()
     own_g = get(g_hbm, g_buf.at[core])
     wire.recv(f_got, f_buf.at[other])
-    wire.recycle(keep=3 * chunks2)
+    wire.recycle(keep=chunks2)
     g_got = wire.send(g_hbm, g_buf.at[core], partner)
     for chunk in range(chunks2):
         y_gathers[chunk].finish()
@@ -520,7 +526,10 @@
     wire.recv_all(groups, rr.at[:, :, :, z])
 
     r_gathers = [
-        DirectGather(wire, z_ring, lambda place, q=q: rr.at[q, :, :, place]) for q in range(2)
+        DirectGather(
+            wire, z_ring, lambda place, q=q: rr.at[q, :, :, place], lambda q=q: rr.at[q, :, :, pl.ds(0, 3)]
+        )
+        for q in range(2)
     ]
     for q in range(2):
         r_gathers[q].start()

time: 76.9 us -> 76.7 us (level)
  no operation moved by 1% of the time
where the time goes in v6:
time: 76.7 us; the launch traced here: 76.6 us
  Pallas kernels  74.6 us (97%)
  local copies, waits for them, and re-layouts  1.33 us (2%)
    pallas_call x1, Pallas kernels, local(): pl.pallas_call(kernel, out_shape=shapes, in_specs=[far] * 6, out_specs=(w...  74.6 us

profile of v6, /device:TPU:0, one launch (start us, length us, event | category | flops | bytes accessed | tf_op | source)
XLA Modules:
  0.0 76.6 jit_solution(15022338769627992893)
XLA Ops:
  0.6 74.6 %shard_map.77 = (bf16[2,64,512]{2,1,0:T(8,128)(2,1)S(1)}, f32[2,16,1536]{2,1,0:T(8,128)S(1)}) custom-call(bf16[2,16,2048]{2,1,0:T(8,128)(2,1)} %bitcast.5, bf16[2,2048,512]{2,1,0:T(8,128)(2,1)} %a_hbm.1, bf16[2,2048,512]{2,1,0:T(8,128)(2,1)} %f_hbm.1, s32[2,64]{1,0:T(2,128)} %lists_hbm.1, bf16[2,768,256]{2,1,0:T(8,128)(2,1)} %rhs_hbm.1, ...), custom_call_target="tpu_custom_call" | custom-call | tf_op jit(solution)/shard_map/pallas_call | solution.py:649
  75.3 0.7 copy.10
  75.9 0.7 copy.11
